TPU v7x, 256 devices: a whole 4x4x8 slice. The times are simulated.
256 devices in a mesh: row: 8 (over z_hi, x), col: 32 (over y, z_lo, core).
Axes of the slice: x: 4, y: 4, z: 8 (z_hi: 2, z_lo: 4; z = z_hi * 4 + z_lo), core: 2. Of those that a mesh axis runs over, the one named last changes fastest.
Arguments:
- prior_cov: float32 [16384, 16384], P('row', 'col'), as said below
- diffusivity: float32 [16384], replicated, may hold values from 0.05 to 0.2
- velocity: float32 [2, 16384], replicated, may hold values from -0.3 to 0.3
- process_noise_variance: float32 [16384], replicated, may hold values from 0.2 to 1
- observed_index: int32 [256], replicated, may hold values from 0 to 16383, as said below
- innov_factor: float32 [256, 256], replicated, may hold values from -0.048 to 1.048
Outputs:
- analysis_cov: float32 [16384, 16384], P('row', 'col')
Inputs may be any that keep to these rules, and one draw needn't show every extreme that they name: `prior_cov`: symmetric positive definite. `observed_index`: 256 distinct point indices.
All inputs are finite; a program needn't handle non-finite values.
Results may differ from a plain program's by a relative error of at most 0.000098.
Values sent between devices are 32-bit elements; how exact they have to be, the bound alone decides.
A program may use at most 128 MiB of HBM per device.

v0:
```python
import jax
import jax.numpy as jnp
from jax import lax
from jax.sharding import PartitionSpec as P

GY = 128
STEPS = 2


def with_halo(shard, sides, width):
    for axis, dim in sides:
        peers, length = (lax.axis_size(axis), shard.shape[dim])
        up = [(i, (i + 1) % peers) for i in range(peers - 1)]
        down = [(j, i) for i, j in up]
        last = lax.slice_in_dim(shard, length - width, length, axis=dim)
        leading = lax.slice_in_dim(shard, 0, width, axis=dim)
        before = lax.ppermute(last, axis, up)
        after = lax.ppermute(leading, axis, down)
        shard = jnp.concatenate([before, shard, after], axis=dim)
    return shard


def advect(values, diffuse_coef, east_speed, south_speed, grid_axis):
    extent = values.shape[grid_axis]
    north_side = lax.slice_in_dim(values, 0, extent - 2, axis=grid_axis)
    center = lax.slice_in_dim(values, 1, extent - 1, axis=grid_axis)
    south_side = lax.slice_in_dim(values, 2, extent, axis=grid_axis)
    span_cols = values.shape[grid_axis + 1]
    zero_edge = jnp.zeros_like(lax.slice_in_dim(center, 0, 1, axis=grid_axis + 1))
    east_side = jnp.concatenate(
        [lax.slice_in_dim(center, 1, span_cols, axis=grid_axis + 1), zero_edge], axis=grid_axis + 1
    )
    west_side = jnp.concatenate(
        [zero_edge, lax.slice_in_dim(center, 0, span_cols - 1, axis=grid_axis + 1)],
        axis=grid_axis + 1,
    )
    laplace = north_side + south_side + east_side + west_side - 4.0 * center
    return (
        center
        + diffuse_coef * laplace
        - 0.5 * east_speed * (east_side - west_side)
        - 0.5 * south_speed * (south_side - north_side)
    )


def on_device(
    prior_cov, diffusivity, velocity, process_noise_variance, observed_index, innov_factor
):
    top_precision = lax.Precision.HIGHEST
    rows_dev, cols_dev = prior_cov.shape
    row_start = lax.axis_index("row") * rows_dev
    col_start = lax.axis_index("col") * cols_dev
    margin = GY * STEPS
    diffuse_pad = jnp.pad(diffusivity, (margin, margin))
    east_pad = jnp.pad(velocity[0], (margin, margin))
    south_pad = jnp.pad(velocity[1], (margin, margin))

    def window(offset, amount, shaped):
        return tuple(
            (
                lax.dynamic_slice_in_dim(table, offset + margin, amount).reshape(shaped)
                for table in (diffuse_pad, east_pad, south_pad)
            )
        )

    present_state = prior_cov
    coefs = window(row_start, rows_dev, (rows_dev // GY, GY, 1))
    for substep in range(STEPS):
        widened = with_halo(present_state, (("row", 0),), GY)
        present_state = advect(
            widened.reshape(-1, GY, cols_dev), coefs[0], coefs[1], coefs[2], 0
        ).reshape(rows_dev, cols_dev)
    coefs = window(col_start, cols_dev, (1, cols_dev // GY, GY))
    for substep in range(STEPS):
        widened = with_halo(present_state, (("col", 1),), GY)
        present_state = advect(
            widened.reshape(rows_dev, -1, GY), coefs[0], coefs[1], coefs[2], 1
        ).reshape(rows_dev, cols_dev)
    row_labels = row_start + lax.iota(jnp.int32, rows_dev)
    column_labels = col_start + lax.iota(jnp.int32, cols_dev)
    variance_rows = lax.dynamic_slice_in_dim(process_noise_variance, row_start, rows_dev)
    predicted_cov = present_state + jnp.where(
        row_labels[:, None] == column_labels[None, :], variance_rows[:, None], 0.0
    )
    pick_cols = (column_labels[:, None] == observed_index[None, :]).astype(jnp.float32)
    pick_rows = (row_labels[:, None] == observed_index[None, :]).astype(jnp.float32)
    stencil_weights = jnp.dot(
        pick_cols, innov_factor.T, precision=top_precision, preferred_element_type=jnp.float32
    )
    partial_left_product = jnp.dot(
        predicted_cov, stencil_weights, precision=top_precision, preferred_element_type=jnp.float32
    )
    left_multiplier = lax.psum(partial_left_product, "col")
    observed = lax.dot_general(
        pick_rows,
        predicted_cov,
        (((0,), (0,)), ((), ())),
        precision=top_precision,
        preferred_element_type=jnp.float32,
    )
    observed = lax.psum(observed, "row")
    right_multiplier = jnp.dot(
        innov_factor, observed, precision=top_precision, preferred_element_type=jnp.float32
    )
    return predicted_cov - jnp.dot(
        left_multiplier,
        right_multiplier,
        precision=top_precision,
        preferred_element_type=jnp.float32,
    )


def solution(mesh):
    return jax.shard_map(
        on_device,
        mesh=mesh,
        in_specs=(P("row", "col"), P(), P(), P(), P(), P()),
        out_specs=P("row", "col"),
        check_vma=False,
    )
```

profile of v0, /device:TPU:2, one launch (start us, length us, event | category | flops | bytes accessed | tf_op | source)
XLA Modules:
  0.0 592.1 jit_solution(15418751431844451939)
XLA Ops:
  6.5 0.0 copy-start
  6.5 1.1 fusion.40
  7.6 3.4 collective-permute-start
  11.1 2.5 collective-permute-start.1
  13.5 1.1 fusion.41
  14.6 5.4 copy.11
  20.0 7.9 %fusion.39 = (f32[16,127,512]{1,0,2:T(8,128)}, f32[16,127,512]{1,0,2:T(8,128)}) fusion(f32[16,128,512]{1,0,2:T(8,128)} %copy.11), kind=kLoop, calls=%fused_computation.66 | loop fusion | bytes 16646144 | tf_op jit(solution)/shard_map/slice | solution.py:31
  28.0 0.1 fusion.29
  28.0 0.1 fusion.25
  28.1 0.0 collective-permute-done
  28.1 0.0 collective-permute-done.1
  28.1 7.7 %fusion.6 = (f32[2048,512]{1,0:T(8,128)}, f32[2048,512]{1,0:T(8,128)}) fusion(f32[2048,512]{1,0:T(8,128)} %param.6, f32[128,512]{1,0:T(8,128)S(1)} %collective-permute-done, f32[128,512]{1,0:T(8,128)S(1)} %collective-permute-done.1), kind=kLoop, calls=%fused_computation.22 | loop fusion | flops 4194304 | bytes 13107200 | tf_op jit(solution)/shard_map/add | solution.py:37
  35.8 5.4 copy.12
  41.2 5.4 copy.8
  46.7 8.1 %multiply_subtract_fusion.2 = f32[16,128,512]{1,0,2:T(8,128)S(1)} fusion(f32[16,128,512]{1,0,2:T(8,128)} %copy.12, f32[16,128,512]{1,0,2:T(8,128)} %copy.11, f32[16,127,512]{1,0,2:T(8,128)} %get-tuple-element.22, f32[16,128,512]{1,0,2:T(8,128)} %copy.8, f32[16,127,512]{1,0,2:T(8,128)} %get-tuple-element.21, f32[16,128]{1,0:T(8,128)S(1)} %fusion.29, ...), kind=kLoop, calls=%fused_computation.21 | loop fusion | flops 11534336 | bytes 25124864 | tf_op jit(solution)/shard_map/sub | solution.py:39
  54.7 0.4 fusion.38
  55.1 3.4 collective-permute-start.2
  58.5 2.6 collective-permute-start.3
  61.2 3.4 fusion.37
  64.5 2.0 copy.22
  66.5 0.0 collective-permute-done.2
  66.5 5.9 %collective-permute-done.3 = f32[128,512]{0,1:T(8,128)S(1)} collective-permute-done((f32[128,512]{0,1:T(8,128)S(1)}, f32[128,512]{0,1:T(8,128)S(1)}, u32[]{:S(2)}, u32[]{:S(2)}) %collective-permute-start.3) | collective-permute-done | bytes 262176 | tf_op jit(solution)/shard_map/ppermute | solution.py:18
  72.4 1.1 add_bitcast_fusion
  73.6 0.9 copy.16
  74.5 0.0 copy-start.3
  74.5 0.9 copy.17
  75.5 1.2 copy-done.3
  76.7 2.7 fusion
  79.4 2.0 copy.21
  81.4 0.0 copy-start.1
  81.4 2.0 copy-done.1
  83.4 1.2 fusion.36
  84.6 1.3 collective-permute-start.4
  86.0 1.5 collective-permute-start.5
  87.5 0.8 fusion.30
  88.3 0.1 multiply_bitcast_fusion
  88.4 0.0 collective-permute-done.4
  88.4 7.6 %collective-permute-done.5 = f32[2048,128]{0,1:T(8,128)S(1)} collective-permute-done((f32[2048,128]{0,1:T(8,128)S(1)}, f32[2048,128]{0,1:T(8,128)S(1)}, u32[]{:S(2)}, u32[]{:S(2)}) %collective-permute-start.5) | collective-permute-done | bytes 1048608 | tf_op jit(solution)/shard_map/ppermute | solution.py:18
  96.0 2.6 pad_maximum_fusion
  98.6 1.2 fusion.34
  99.8 2.7 multiply_subtract_fusion.1
  102.6 0.0 copy-start.2
  102.6 2.0 copy-done.2
  104.6 1.2 fusion.35
  105.8 21.7 %collective-permute-start.6 = (f32[2048,128]{0,1:T(8,128)}, f32[2048,128]{0,1:T(8,128)S(1)}, u32[]{:S(2)}, u32[]{:S(2)}) collective-permute-start(f32[2048,128]{0,1:T(8,128)} %get-tuple-element.13), channel_id=1, source_target_pairs={{0,1},{1,2},{2,3},{3,4},{4,5},{5,6},{6,7},{7,8},{8,9},{9,10},{10,1... | collective-permute-start | bytes 3145736 | tf_op jit(solution)/shard_map/ppermute | solution.py:17
  127.5 1.3 collective-permute-start.7
  128.8 0.7 dynamic_slice.27
  129.5 0.4 collective-permute-done.6
  129.9 2.1 collective-permute-done.7
  132.0 2.6 pad_maximum_fusion.1
  134.7 1.2 fusion.33
  135.9 4.1 multiply_subtract_fusion
  140.0 5.3 copy.14
  145.3 6.1 %fusion.8 = f32[256,512]{1,0:T(8,128)} fusion(f32[2048,512]{1,0:T(8,128)} %copy.14, f32[2048]{0:T(1024)S(1)} %dynamic_slice.27, s32[512]{0:T(512)S(1)} %iota_add_fusion.1, s32[2048]{0:T(1024)S(1)} %iota_add_fusion, s32[256]{0:T(256)S(1)} %copy-done.5), kind=kOutput, calls=%fused_computation.25 | convolution fusion | flops 3224895488 | bytes 4738048 | tf_op jit(solution)/shard_map/dot_general | solution.py:94
  151.4 0.0 all-reduce.16.cloned.1.call-update
  151.5 0.3 all-reduce.14.cloned.1.call-start
  151.8 0.0 copy-done
  151.8 0.4 fusion.21
  152.2 7.2 %fusion.9 = f32[2048,256]{1,0:T(8,128)} fusion(f32[512,256]{1,0:T(8,128)S(1)} %fusion.21, f32[2048,512]{1,0:T(8,128)} %copy.14, f32[2048]{0:T(1024)S(1)} %dynamic_slice.27, s32[512]{0:T(512)S(1)} %iota_add_fusion.1, s32[2048]{0:T(1024)S(1)} %iota_add_fusion), kind=kOutput, calls=%fused_computation.26 | convolution fusion | flops 3224371200 | bytes 6834176 | tf_op jit(solution)/shard_map/dot_general | solution.py:90
  159.4 0.0 all-reduce.14.cloned.1.call-update
  159.4 129.7 %all-reduce.16.cloned.1.call-done = f32[256,512]{1,0:T(8,128)} async-done(((f32[256,512]{1,0:T(8,128)}), f32[256,512]{1,0:T(8,128)}) %all-reduce.16.cloned.1.call-update) | async-done | bytes 524304 | tf_op jit(solution)/shard_map/psum | solution.py:101
  289.1 2.0 fusion.42
  291.2 285.3 %all-reduce.14.cloned.1.call-done = f32[2048,256]{1,0:T(8,128)} async-done(((f32[2048,256]{1,0:T(8,128)}), f32[2048,256]{1,0:T(8,128)}) %all-reduce.14.cloned.1.call-update) | async-done | bytes 2097168 | tf_op jit(solution)/shard_map/psum | solution.py:93
  576.5 8.7 %convolution_subtract_fusion = f32[2048,512]{1,0:T(8,128)} fusion(f32[2048,256]{1,0:T(8,128)} %all-reduce.14.cloned.1.call-done, f32[512,256]{1,0:T(8,128)S(1)} %fusion.42, f32[2048,512]{1,0:T(8,128)} %copy.14, f32[2048]{0:T(1024)S(1)} %dynamic_slice.27, s32[512]{0:T(512)S(1)} %iota_add_fusion.1, s32[2048]{0:T(1024)S(1)} %iota_add_fusion), kind=kOutput, calls=%fused_computation.24 | convolution fusion | flops 3225419776 | bytes 11028480 | tf_op jit(solution)/shard_map/dot_general | solution.py:105
  (7 shorter events, 0.0 us)
Async XLA Ops:
  6.5 145.2 %copy-start = (f32[256,256]{1,0:T(8,128)S(1)}, f32[256,256]{1,0:T(8,128)}, u32[]{:S(2)}) copy-start(f32[256,256]{1,0:T(8,128)} %param.11) | copy-start | bytes 786436
  6.5 282.6 %all-reduce.16.cloned.1.call-start = ((), (), s32[]{:S(2)}) async-start(), calls=%async_computation.1 | async-start | bytes 1048576 | tf_op jit(solution)/shard_map/psum | solution.py:101
  7.6 20.5 %collective-permute-start = (f32[128,512]{1,0:T(8,128)S(1)}, f32[128,512]{1,0:T(8,128)S(1)}, u32[]{:S(2)}, u32[]{:S(2)}) collective-permute-start(f32[128,512]{1,0:T(8,128)S(1)} %get-tuple-element.24), channel_id=1, source_target_pairs={{0,32},{32,64},{64,96},{96,128},{128,160},{160,192},{192,224},{1,3... | collective-permute-start | bytes 786440 | tf_op jit(solution)/shard_map/ppermute | solution.py:17
  11.1 17.1 %collective-permute-start.1 = (f32[128,512]{1,0:T(8,128)S(1)}, f32[128,512]{1,0:T(8,128)S(1)}, u32[]{:S(2)}, u32[]{:S(2)}) collective-permute-start(f32[128,512]{1,0:T(8,128)S(1)} %get-tuple-element.23), channel_id=1, source_target_pairs={{32,0},{64,32},{96,64},{128,96},{160,128},{192,160},{224,192},{33,... | collective-permute-start | bytes 786440 | tf_op jit(solution)/shard_map/ppermute | solution.py:18
  20.0 8.0 %copy-start.4 = (f32[16384]{0:T(1024)S(1)}, f32[16384]{0:T(1024)}, u32[]{:S(2)}) copy-start(f32[16384]{0:T(1024)} %param.7) | copy-start | bytes 196612
  55.1 11.4 %collective-permute-start.2 = (f32[128,512]{0,1:T(8,128)S(1)}, f32[128,512]{0,1:T(8,128)S(1)}, u32[]{:S(2)}, u32[]{:S(2)}) collective-permute-start(f32[128,512]{0,1:T(8,128)S(1)} %bitcast.87), channel_id=1, source_target_pairs={{0,32},{32,64},{64,96},{96,128},{128,160},{160,192},{192,224},{1,3... | collective-permute-start | bytes 786440 | tf_op jit(solution)/shard_map/ppermute | solution.py:17
  58.5 13.9 %collective-permute-start.3 = (f32[128,512]{0,1:T(8,128)S(1)}, f32[128,512]{0,1:T(8,128)S(1)}, u32[]{:S(2)}, u32[]{:S(2)}) collective-permute-start(f32[128,512]{0,1:T(8,128)S(1)} %bitcast.86), channel_id=1, source_target_pairs={{32,0},{64,32},{96,64},{128,96},{160,128},{192,160},{224,192},{33,... | collective-permute-start | bytes 786440 | tf_op jit(solution)/shard_map/ppermute | solution.py:18
  74.5 2.2 copy-start.3
  81.4 2.0 copy-start.1
  84.6 3.8 collective-permute-start.4
  86.0 10.0 %collective-permute-start.5 = (f32[2048,128]{0,1:T(8,128)S(1)}, f32[2048,128]{0,1:T(8,128)S(1)}, u32[]{:S(2)}, u32[]{:S(2)}) collective-permute-start(f32[2048,128]{0,1:T(8,128)S(1)} %get-tuple-element.16), channel_id=1, source_target_pairs={{1,0},{2,1},{3,2},{4,3},{5,4},{6,5},{7,6},{8,7},{9,8},{10,9},{11,1... | collective-permute-start | bytes 3145736 | tf_op jit(solution)/shard_map/ppermute | solution.py:18
  102.6 2.0 copy-start.2
  105.8 24.1 %collective-permute-start.6 = (f32[2048,128]{0,1:T(8,128)}, f32[2048,128]{0,1:T(8,128)S(1)}, u32[]{:S(2)}, u32[]{:S(2)}) collective-permute-start(f32[2048,128]{0,1:T(8,128)} %get-tuple-element.13), channel_id=1, source_target_pairs={{0,1},{1,2},{2,3},{3,4},{4,5},{5,6},{6,7},{7,8},{8,9},{9,10},{10,1... | collective-permute-start | bytes 3145736 | tf_op jit(solution)/shard_map/ppermute | solution.py:17
  127.5 4.6 collective-permute-start.7
  140.0 5.3 copy-start.5
  151.5 425.1 %all-reduce.14.cloned.1.call-start = ((), (), s32[]{:S(2)}) async-start(), calls=%async_computation | async-start | bytes 4194304 | tf_op jit(solution)/shard_map/psum | solution.py:93
Sparse Core Ops, SparseCore 0:
  151.6 137.4 all-reduce.15
  291.8 284.7 all-reduce.13
where the time goes:
time: 594 us; the launch traced here: 592 us
  waiting for transfers between devices  431 us (73%)
  local copies, waits for them, and re-layouts  52.8 us (9%)
  starting transfers between devices  38 us (6%)
  other arithmetic  31.9 us (5%)
  matrix products  24.5 us (4%)
  between operations  13.6 us (2%)
    psum x1, waiting for transfers between devices, on_device(): left_multiplier = lax.psum(partial_left_product, 'col')  285 us
    psum x1, waiting for transfers between devices, on_device(): observed = lax.psum(observed, 'row')  130 us
    ppermute x4, starting transfers between devices, with_halo(): before = lax.ppermute(last, axis, up)  29.8 us
    sub x4, other arithmetic, advect(): center + diffuse_coef * laplace - 0.5 * east_speed * (east_side - west_side)  17.6 us
    ppermute x4, waiting for transfers between devices, with_halo(): after = lax.ppermute(leading, axis, down)  15.7 us
    slice x4, local copies, waits for them, and re-layouts, advect(): lax.slice_in_dim(center, 1, span_cols, axis=grid_axis + 1)  13.7 us
  transfers between devices with their start and end apart: 10, of which 6 were waited for; matrix products, arithmetic and copies ran while one was open for 5% of the time, Pallas kernels for 0%

commit v1 on v0

v1 whole, which is shorter than its diff:
```python
import functools

import jax
import jax.numpy as jnp
from jax import lax
from jax.experimental import pallas as pl
from jax.experimental.pallas import tpu as pltpu
from jax.sharding import PartitionSpec as P

GX = 128
GY = 128
NOBS = 256
ROWS = 2048
COLS = 512
LT = 4
F32 = jnp.float32
BF = jnp.bfloat16
MESH = pl.DeviceIdType.MESH
PAD = 8
VM = pl.BlockSpec(memory_space=pltpu.VMEM)
ANY = pl.BlockSpec(memory_space=pl.ANY)


def split2(v):
    hi = v.astype(BF)
    return hi, (v - hi.astype(F32)).astype(BF)


def dot3(a, b, dims):
    (ah, al), (bh, bl) = split2(a), split2(b)
    dg = functools.partial(
        lax.dot_general, dimension_numbers=(dims, ((), ())), preferred_element_type=F32
    )
    return dg(ah, bh) + (dg(ah, bl) + dg(al, bh))


def coefficients(diffusivity, velocity, variance):
    k, a, b = [t.reshape(GX, GY) for t in (diffusivity, velocity[0], velocity[1])]
    q = variance.reshape(GX, GY)
    lane = lax.broadcasted_iota(jnp.int32, (GX, GY), 1)
    center = 1.0 - 4.0 * k
    north = k + 0.5 * b
    south = k - 0.5 * b
    east = jnp.where(lane < GY - 1, k - 0.5 * a, 0.0)
    west = jnp.where(lane > 0, k + 0.5 * a, 0.0)
    zero = jnp.zeros_like(k)
    rows = jnp.stack([center, north, south, east, west, q, zero, zero], axis=1)
    up = jnp.concatenate([zero[:1], south[:-1]], axis=0)
    down = jnp.concatenate([north[1:], zero[:1]], axis=0)
    before = jnp.concatenate([zero[:, :1], east[:, :-1]], axis=1)
    after = jnp.concatenate([west[:, 1:], zero[:, :1]], axis=1)
    turned = jnp.stack([center, up, down, after, before, zero, zero, zero], axis=1)
    pad = ((PAD, PAD), (0, 0), (0, 0))
    return jnp.pad(rows, pad), jnp.pad(turned, pad)


def spread_rows(coef_ref, first, count, out_ref):
    def body(g, _):
        tile = jnp.transpose(coef_ref[first + g])
        for j in range(5):
            out_ref[j, pl.ds(pl.multiple_of(g * GY, GY), GY), :] = jnp.broadcast_to(
                tile[:, j : j + 1], (GY, GY)
            )
        return 0

    lax.fori_loop(0, count, body, 0)


def row_step(src, coef, base, lt, lead):
    at = pl.multiple_of(base + lead, 8)
    mid = src[lt, pl.ds(at, 8), :]
    north = src[lt, pl.ds(pl.multiple_of(at - GY, 8), 8), :]
    south = src[lt, pl.ds(pl.multiple_of(at + GY, 8), 8), :]
    east = src[lt, pl.ds(at + 1, 8), :]
    west = src[lt, pl.ds(at - 1, 8), :]
    return (coef[0] * mid + coef[1] * north) + (coef[2] * south + (coef[3] * east + coef[4] * west))


def col_two_steps(tiles, coef_ref, first):
    def step(v, g):
        c = [coef_ref[first + g, j : j + 1, :] for j in range(5)]
        east = pltpu.roll(v[g], GY - 1, 1)
        west = pltpu.roll(v[g], 1, 1)
        return (c[0] * v[g] + c[1] * v[g - 1]) + (c[2] * v[g + 1] + (c[3] * east + c[4] * west))

    v1 = {g: step(tiles, g) for g in range(-1, 5)}
    return [step(v1, g) for g in range(4)]


def k0(obs_ref, c_ref, turned_ref, t_ref, e_ref, u_ref, spread_ref):
    r = lax.axis_index("row")
    spread_rows(turned_ref, PAD + 16 * r - 1, 18, spread_ref)
    start = r * ROWS - 2 * GY

    def hot(i, _):
        base = pl.multiple_of(i * 8, 8)
        ids = start + base + lax.broadcasted_iota(jnp.int32, (8, GY), 0)
        for lt in range(2):
            e_ref[lt, pl.ds(base, 8), :] = jnp.where(
                ids == obs_ref[:, lt * GY : (lt + 1) * GY], 1.0, 0.0
            )
        return 0

    lax.fori_loop(0, 2560 // 8, hot, 0)

    def one(i, _):
        base = pl.multiple_of(i * 8, 8)
        coef = [spread_ref[j, pl.ds(base, 8), :] for j in range(5)]
        for lt in range(2):
            u_ref[lt, pl.ds(base, 8), :] = row_step(e_ref, coef, base, lt, GY)
        return 0

    lax.fori_loop(0, 2304 // 8, one, 0)

    def two(i, _):
        base = pl.multiple_of(i * 8, 8)
        coef = [spread_ref[j, pl.ds(pl.multiple_of(base + GY, 8), 8), :] for j in range(5)]
        for lt in range(2):
            e_ref[lt, pl.ds(base, 8), :] = row_step(u_ref, coef, base, lt, GY)
        return 0

    lax.fori_loop(0, ROWS // 8, two, 0)

    def gather(i, _):
        base = pl.multiple_of(i * 512, 512)
        c = c_ref[pl.ds(base, 512), :]
        w = jnp.concatenate([e_ref[lt, pl.ds(base, 512), :] for lt in range(2)], axis=1)
        t = dot3(w, c, ((0,), (0,)))
        for lt in range(LT):
            part = t[:, lt * GY : (lt + 1) * GY]
            t_ref[lt] = jnp.where(i == 0, part, t_ref[lt] + part)
        return 0

    for lt in range(LT):
        t_ref[lt] = jnp.zeros((NOBS, GY), F32)
    lax.fori_loop(0, ROWS // 512, gather, 0)


def ka(
    c_ref,
    t_ref,
    rows_ref,
    obs_ref,
    left_ref,
    right_ref,
    edge_ref,
    halo_ref,
    pc_ref,
    pr_ref,
    ext,
    vb,
    pc,
    pr,
    rs,
    zsum,
    zin,
    text,
    relay1,
    relay2,
    send,
    recv,
    local,
):
    r = lax.axis_index("row")
    c = lax.axis_index("col")
    zh, x = r // 4, r % 4
    y, zl, k = c // 8, (c % 8) // 2, c % 2
    x_edge = jnp.where(zh == 0, 3, 0)
    has_left, has_right = c > 0, c < 31
    partner = (4 * (1 - zh) + x, c)
    x_peers = [(4 * zh + (x + d) % 4, c) for d in (1, 2, 3)]
    y_peers = [(r, 8 * ((y + d) % 4) + 2 * zl + k) for d in (1, 2, 3)]
    z_peers = [(r, 8 * y + 2 * ((zl + d) % 4) + k) for d in (1, 2, 3)]
    core = (r, c + 1 - 2 * k)
    x_to = 2 * (y - 2 * zh) + zl // 2
    gives = (y // 2 == zh) & jnp.logical_not((x_to == x) & (y == x))
    keeps = (y // 2 == zh) & (x_to == x) & (y == x)
    give_to = (4 * zh + jnp.where(gives, x_to, x), 8 * x + 2 * zl + k)
    y_from = 2 * zh + x // 2
    holder = zl // 2 == x % 2
    takes = holder & jnp.logical_not((y_from == y) & (x == y))
    take_from = (4 * zh + y, 8 * y_from + 2 * zl + k)

    def remote(src, dst, s, t, device):
        return pltpu.make_async_remote_copy(
            src_ref=src,
            dst_ref=dst,
            send_sem=send.at[s],
            recv_sem=recv.at[t],
            device_id=device,
            device_id_type=MESH,
        )

    barrier = pltpu.get_barrier_semaphore()

    def greet(device):
        pl.semaphore_signal(barrier, inc=1, device_id=device, device_id_type=MESH)

    for device in x_peers + y_peers + z_peers + [partner, core]:
        greet(device)
    left, right = (r, jnp.maximum(c - 1, 0)), (r, jnp.minimum(c + 1, 31))
    pl.when(has_left)(lambda: greet(left))
    pl.when(has_right)(lambda: greet(right))
    pl.when(gives)(lambda: greet(give_to))
    pl.when(takes)(lambda: greet(take_from))
    one = lambda flag: jnp.where(flag, 1, 0)
    pl.semaphore_wait(
        barrier, 11 + one(has_left) + one(has_right) + one(gives) + one(takes)
    )

    def halo_out(side, piece, t):
        col = GY * t + (256 if side == 1 else 0)
        src = c_ref.at[pl.ds((0, 1792, 256)[piece], 1536 if piece == 2 else 256), pl.ds(col, GY)]
        sem = side * 6 + piece * 2 + t
        device = right if side == 1 else left
        if piece == 2:
            dst = (left_ref if side == 1 else right_ref).at[t]
        else:
            dst = ext.at[t + (0 if side == 1 else 6), pl.ds(256 * piece, 256)]
        return remote(src, dst, sem, sem, device)

    flags = {0: (has_left, has_right), 1: (has_right, has_left)}
    for piece in (0, 1):
        for side in (0, 1):

            @pl.when(flags[side][0])
            def _():
                for t in (0, 1):
                    halo_out(side, piece, t).start()

    inner = [
        pltpu.make_async_copy(
            c_ref.at[pl.ds(1792 * h, 256), pl.ds(GY * t, GY)],
            ext.at[2 + t, pl.ds(256 * h, 256)],
            local.at[4 * h + t],
        )
        for h in (0, 1)
        for t in range(LT)
    ]
    for copy in inner:
        copy.start()

    def rs_copy(d):
        there = (x + d + 1) % 4
        return remote(
            t_ref.at[:, pl.ds(pl.multiple_of(64 * there, 64), 64), :],
            rs.at[d],
            12 + d,
            12 + d,
            x_peers[d],
        )

    for d in range(3):
        rs_copy(d).start()
    for side in (0, 1):

        @pl.when(flags[side][0])
        def _():
            for t in (0, 1):
                halo_out(side, 2, t).start()

    for d in range(3):
        rs_copy(d).wait()
    mine = pl.ds(pl.multiple_of(64 * x, 64), 64)
    for lt in range(LT):
        zsum[lt] = (t_ref[lt, mine, :] + rs[0, lt]) + (rs[1, lt] + rs[2, lt])
    z_copy = remote(zsum, zin, 15, 15, partner)
    z_copy.start()

    for copy in inner:
        copy.wait()
    for side, (there, tiles) in {0: (has_right, (6, 7)), 1: (has_left, (0, 1))}.items():

        @pl.when(there)
        def _():
            for piece in (0, 1):
                for t in (0, 1):
                    halo_out(side, piece, t).wait_recv()

        @pl.when(jnp.logical_not(there))
        def _():
            for t in tiles:
                ext[t] = jnp.zeros((512, GY), F32)

    first = PAD + 4 * c

    def edge(i, _):
        at = pl.ds(pl.multiple_of(i * 16, 16), 16)
        out = col_two_steps({g - 2: ext[g, at, :] for g in range(8)}, rows_ref, first)
        for lt in range(LT):
            vb[lt, at, :] = out[lt]
        return 0

    lax.fori_loop(0, 512 // 16, edge, 0)
    edge_out = pltpu.make_async_copy(vb, edge_ref, local.at[8])
    edge_out.start()

    top, bottom = pl.ds(0, 256), pl.ds(256, 256)
    up_near, down_near = x > 0, x < 3
    up_to = (4 * zh + jnp.maximum(x - 1, 0), c)
    down_to = (4 * zh + jnp.minimum(x + 1, 3), c)
    up_copy = remote(vb.at[:, top], halo_ref.at[:, bottom], 16, 16, up_to)
    down_copy = remote(vb.at[:, bottom], halo_ref.at[:, top], 17, 17, down_to)
    pl.when(up_near)(lambda: up_copy.start())
    pl.when(down_near)(lambda: down_copy.start())
    at_edge = x == x_edge
    far = (4 * zh + x_edge, c)
    cross = pl.ds(pl.multiple_of(jnp.where(zh == 0, 256, 0), 256), 256)
    hop1 = [
        (j, remote(vb.at[j, cross], relay1, 18 + j, 18, (4 * zh + j, c))) for j in range(4)
    ]
    keep1 = pltpu.make_async_copy(vb.at[x, cross], relay1, local.at[9])

    @pl.when(at_edge)
    def _():
        for j, copy in hop1:
            pl.when(x != j)(lambda copy=copy: copy.start())
        keep1.start()

    z_copy.wait()
    for lt in range(LT):
        text[2 + lt] = zsum[lt] + zin[lt]
    t_right = remote(text.at[pl.ds(4, 2)], text.at[pl.ds(0, 2)], 22, 22, right)
    t_left = remote(text.at[pl.ds(2, 2)], text.at[pl.ds(6, 2)], 23, 23, left)
    pl.when(has_right)(lambda: t_right.start())
    pl.when(has_left)(lambda: t_left.start())

    hop2 = remote(relay1, relay2, 24, 24, partner)
    pl.when(at_edge)(lambda: keep1.wait())
    pl.when(jnp.logical_not(at_edge))(lambda: hop1[0][1].wait_recv())
    hop2.start()

    for there, copy, tiles in ((has_left, t_right, (0, 1)), (has_right, t_left, (6, 7))):
        pl.when(there)(lambda copy=copy: copy.wait_recv())

        @pl.when(jnp.logical_not(there))
        def _():
            for t in tiles:
                text[t] = jnp.zeros((64, GY), F32)

    my_obs = obs_ref[mine, :]
    for h in range(4):
        at = pl.ds(16 * h, 16)
        out = col_two_steps({g - 2: text[g, at, :] for g in range(8)}, rows_ref, first)
        for lt in range(LT):
            ids = c * COLS + lt * GY + lax.broadcasted_iota(jnp.int32, (16, GY), 1)
            noise = jnp.broadcast_to(rows_ref[first + lt, 5:6, :], (16, GY))
            zsum[lt, at, :] = out[lt] + jnp.where(my_obs[16 * h : 16 * h + 16] == ids, noise, 0.0)
    p_copy = [remote(zsum, pc.at[:, mine], 25 + d, 25 + d, x_peers[d]) for d in range(3)]
    for copy in p_copy:
        copy.start()
    mine_y = pl.ds(pl.multiple_of(64 * y, 64), 64)
    s = zl % 2
    a_copy = remote(zsum, pr.at[k, s, :, mine], 28, 28, give_to)
    a_keep = pltpu.make_async_copy(zsum, pr.at[k, s, :, mine], local.at[10])
    pl.when(gives)(lambda: a_copy.start())
    pl.when(keeps)(lambda: a_keep.start())
    for lt in range(LT):
        pc[lt, mine, :] = zsum[lt]

    piece = pr.at[k, s, :, mine_y]
    b_copy = [remote(piece, piece, 29 + d, 29 + s, z_peers[d]) for d in range(3)]
    a_wait = remote(zsum, piece, 28, 28, give_to)

    @pl.when(holder)
    def _():
        pl.when(takes)(lambda: a_wait.wait_recv())
        pl.when(jnp.logical_not(takes))(lambda: a_keep.wait())
        for copy in b_copy:
            copy.start()

    for t in range(2):
        other = pr.at[k, t, :, mine_y]
        arrive = remote(other, other, 29, 29 + t, z_peers[0])
        pl.when(jnp.logical_not(holder & (s == t)))(lambda arrive=arrive: arrive.wait_recv())

    hop3 = remote(relay2, halo_ref.at[x, into2(zh)], 38, 38 + 0, far)
    hop2.wait_recv()
    last = pltpu.make_async_copy(relay2, halo_ref.at[x, into2(zh)], local.at[11])
    pl.when(at_edge)(lambda: last.start())

    def forward(j):
        return remote(relay2, halo_ref.at[j, into2(zh)], 38, 38 + j, far)

    for j in range(4):

        @pl.when(jnp.logical_not(at_edge) & (x == j))
        def _():
            forward(j).start()

    slab = pr.at[k, :, :, mine_y]
    c_copy = [remote(slab, slab, 32 + d, 32 + d, y_peers[d]) for d in range(3)]
    for copy in c_copy:
        copy.start()
    for d in range(3):
        there = pl.ds(pl.multiple_of(64 * ((y + 3 - d) % 4), 64), 64)
        slab_in = pr.at[k, :, :, there]
        remote(slab_in, slab_in, 32 + d, 32 + d, y_peers[d]).wait_recv()
    d_copy = remote(pr.at[k], pr.at[k], 35, 35, core)
    d_copy.start()
    for copy in p_copy:
        copy.wait_recv()
    pc_out = pltpu.make_async_copy(pc, pc_ref, local.at[12])
    pc_out.start()
    other = pr.at[1 - k]
    remote(other, other, 35, 35, core).wait_recv()
    pr_out = pltpu.make_async_copy(pr, pr_ref, local.at[13])
    pr_out.start()

    edge_out.wait()
    pl.when(up_near)(lambda: up_copy.wait_send())
    pl.when(down_near)(lambda: down_copy.wait_send())
    pl.when(down_near)(lambda: up_copy.wait_recv())
    pl.when(up_near)(lambda: down_copy.wait_recv())

    @pl.when(at_edge)
    def _():
        for j, copy in hop1:
            pl.when(x != j)(lambda copy=copy: copy.wait_send())
        last.wait()
        for j in range(4):
            pl.when(x != j)(lambda j=j: forward(j).wait_recv())

    hop2.wait_send()
    pl.when(jnp.logical_not(at_edge))(lambda: hop3.wait_send())
    pl.when(has_right)(lambda: t_right.wait_send())
    pl.when(has_left)(lambda: t_left.wait_send())
    for copy in p_copy:
        copy.wait_send()
    pl.when(gives)(lambda: a_copy.wait_send())
    pl.when(keeps & jnp.logical_not(holder))(lambda: a_keep.wait())

    @pl.when(holder)
    def _():
        for copy in b_copy:
            copy.wait_send()

    for copy in c_copy + [d_copy]:
        copy.wait_send()
    for side in (0, 1):
        out_there, in_there = flags[side]

        @pl.when(out_there)
        def _():
            for piece in (0, 1, 2):
                for t in (0, 1):
                    halo_out(side, piece, t).wait_send()

        @pl.when(in_there)
        def _():
            for t in (0, 1):
                halo_out(side, 2, t).wait_recv()

    pc_out.wait()
    pr_out.wait()


def into2(zh):
    return pl.ds(pl.multiple_of(jnp.where(zh == 0, 256, 0), 256), 256)


def kd(
    pc_ref,
    pr_ref,
    f_ref,
    rows_ref,
    c_ref,
    left_ref,
    right_ref,
    edge_ref,
    halo_ref,
    o_ref,
    ext,
    v,
    v1,
    spread_ref,
    out,
    sem,
    osem,
):
    r = lax.axis_index("row")
    c = lax.axis_index("col")
    copies = [
        pltpu.make_async_copy(
            c_ref.at[pl.ds(256, 1536), pl.ds(GY * t, GY)], ext.at[2 + t], sem.at[t]
        )
        for t in range(LT)
    ]
    copies.append(
        pltpu.make_async_copy(edge_ref.at[:, pl.ds(0, 256)], v.at[:, pl.ds(256, 256)], sem.at[4])
    )
    copies.append(
        pltpu.make_async_copy(
            edge_ref.at[:, pl.ds(256, 256)], v.at[:, pl.ds(2048, 256)], sem.at[5]
        )
    )
    for copy in copies:
        copy.start()
    guarded = [
        (c > 0, left_ref, ext.at[pl.ds(0, 2)], sem.at[6]),
        (c < 31, right_ref, ext.at[pl.ds(6, 2)], sem.at[7]),
        (r > 0, halo_ref.at[:, pl.ds(0, 256)], v.at[:, pl.ds(0, 256)], sem.at[8]),
        (r < 7, halo_ref.at[:, pl.ds(256, 256)], v.at[:, pl.ds(2304, 256)], sem.at[9]),
    ]
    for flag, src, dst, s in guarded:

        @pl.when(flag)
        def _():
            pltpu.make_async_copy(src, dst, s).start()

        @pl.when(jnp.logical_not(flag))
        def _():
            dst[...] = jnp.zeros(dst.shape, F32)

    f = f_ref[...]
    g = dot3(f, f, ((0,), (0,)))
    pc = jnp.concatenate([pc_ref[lt] for lt in range(LT)], axis=1)
    w = dot3(g, pc, ((1,), (0,)))
    for ci in range(4):
        lhs = jnp.concatenate([pr_ref[ci % 2, ci // 2, lt] for lt in range(LT)], axis=1)
        u = dot3(lhs, w, ((0,), (0,)))
        for lt in range(LT):
            out[lt, pl.ds(512 * ci, 512), :] = u[:, lt * GY : (lt + 1) * GY]
    spread_rows(rows_ref, PAD + 16 * r - 1, 18, spread_ref)

    for copy in copies:
        copy.wait()
    for flag, src, dst, s in guarded:

        @pl.when(flag)
        def _():
            pltpu.make_async_copy(src, dst, s).wait()

    first = PAD + 4 * c

    def side(i, _):
        at = pl.ds(pl.multiple_of(i * 16, 16), 16)
        res = col_two_steps({g - 2: ext[g, at, :] for g in range(8)}, rows_ref, first)
        for lt in range(LT):
            v[lt, pl.ds(pl.multiple_of(i * 16 + 512, 16), 16), :] = res[lt]
        return 0

    lax.fori_loop(0, 1536 // 16, side, 0)

    def one(i, _):
        base = pl.multiple_of(i * 8, 8)
        coef = [spread_ref[j, pl.ds(base, 8), :] for j in range(5)]
        for lt in range(LT):
            v1[lt, pl.ds(base, 8), :] = row_step(v, coef, base, lt, GY)
        return 0

    lax.fori_loop(0, 2304 // 8, one, 0)

    def store(n):
        return [
            pltpu.make_async_copy(
                out.at[lt, pl.ds(pl.multiple_of(n * 256, 256), 256)],
                o_ref.at[pl.ds(pl.multiple_of(n * 256, 256), 256), pl.ds(GY * lt, GY)],
                osem.at[n, lt],
            )
            for lt in range(LT)
        ]

    def block(n, _):
        def two(i, _):
            base = pl.multiple_of(n * 256 + i * 8, 8)
            coef = [spread_ref[j, pl.ds(pl.multiple_of(base + GY, 8), 8), :] for j in range(5)]
            for lt in range(LT):
                at = pl.ds(base, 8)
                out[lt, at, :] = row_step(v1, coef, base, lt, GY) - out[lt, at, :]
            return 0

        lax.fori_loop(0, 256 // 8, two, 0)

        @pl.when((c // 4 == r) & (n // 2 == c % 4))
        def _():
            i0 = lax.broadcasted_iota(jnp.int32, (GY, GY), 0)
            i1 = lax.broadcasted_iota(jnp.int32, (GY, GY), 1)
            for h in range(2):
                lt = 2 * (n % 2) + h
                at = pl.ds(pl.multiple_of(n * 256 + h * GY, GY), GY)
                noise = jnp.broadcast_to(rows_ref[first + lt, 5:6, :], (GY, GY))
                out[lt, at, :] = out[lt, at, :] + jnp.where(i0 == i1, noise, 0.0)

        for copy in store(n):
            copy.start()
        return 0

    lax.fori_loop(0, ROWS // 256, block, 0)
    for n in range(ROWS // 256):
        for copy in store(n):
            copy.wait()


def on_device(prior_cov, diffusivity, velocity, variance, observed_index, innov_factor):
    rows, turned = coefficients(diffusivity, velocity, variance)
    shape = jax.ShapeDtypeStruct
    limit = 60 * 1024 * 1024
    partial = pl.pallas_call(
        k0,
        out_shape=shape((LT, NOBS, GY), F32),
        in_specs=[VM] * 3,
        out_specs=VM,
        scratch_shapes=[
            pltpu.VMEM((2, 2560, GY), F32),
            pltpu.VMEM((2, 2304, GY), F32),
            pltpu.VMEM((5, 2304, GY), F32),
        ],
        compiler_params=pltpu.CompilerParams(vmem_limit_bytes=limit),
        name="observe",
    )(observed_index.reshape(1, NOBS), prior_cov, turned)
    left, right, edge, halo, pc, pr = pl.pallas_call(
        ka,
        out_shape=[
            shape((2, 1536, GY), F32),
            shape((2, 1536, GY), F32),
            shape((LT, 512, GY), F32),
            shape((LT, 512, GY), F32),
            shape((LT, NOBS, GY), F32),
            shape((2, 2, LT, NOBS, GY), F32),
        ],
        in_specs=[ANY, VM, VM, VM],
        out_specs=[ANY] * 6,
        scratch_shapes=[
            pltpu.VMEM((8, 512, GY), F32),
            pltpu.VMEM((LT, 512, GY), F32),
            pltpu.VMEM((LT, NOBS, GY), F32),
            pltpu.VMEM((2, 2, LT, NOBS, GY), F32),
            pltpu.VMEM((3, LT, 64, GY), F32),
            pltpu.VMEM((LT, 64, GY), F32),
            pltpu.VMEM((LT, 64, GY), F32),
            pltpu.VMEM((8, 64, GY), F32),
            pltpu.VMEM((256, GY), F32),
            pltpu.VMEM((256, GY), F32),
            pltpu.SemaphoreType.DMA((40,)),
            pltpu.SemaphoreType.DMA((42,)),
            pltpu.SemaphoreType.DMA((14,)),
        ],
        compiler_params=pltpu.CompilerParams(
            collective_id=0, has_side_effects=True, vmem_limit_bytes=limit
        ),
        name="exchange",
    )(prior_cov, partial, rows, observed_index.reshape(NOBS, 1))
    return pl.pallas_call(
        kd,
        out_shape=shape((ROWS, COLS), F32),
        in_specs=[VM, VM, VM, VM] + [ANY] * 5,
        out_specs=ANY,
        scratch_shapes=[
            pltpu.VMEM((8, 1536, GY), F32),
            pltpu.VMEM((LT, 2560, GY), F32),
            pltpu.VMEM((LT, 2304, GY), F32),
            pltpu.VMEM((5, 2304, GY), F32),
            pltpu.VMEM((LT, ROWS, GY), F32),
            pltpu.SemaphoreType.DMA((10,)),
            pltpu.SemaphoreType.DMA((ROWS // 256, LT)),
        ],
        compiler_params=pltpu.CompilerParams(vmem_limit_bytes=limit),
        name="update",
    )(pc, pr, innov_factor, rows, prior_cov, left, right, edge, halo)


def solution(mesh):
    return jax.shard_map(
        on_device,
        mesh=mesh,
        in_specs=(P("row", "col"), P(), P(), P(), P(), P()),
        out_specs=P("row", "col"),
        check_vma=False,
    )
```

time: 594 us -> 178 us (0.30)
  the two profiles are of different devices: /device:TPU:2 before, /device:TPU:225 now
where the time goes in v1:
time: 178 us; the launch traced here: 177 us
  Pallas kernels  168 us (94%)
  local copies, waits for them, and re-layouts  4.92 us (3%)
  other arithmetic  4.35 us (2%)
    pallas_call x1, Pallas kernels, on_device(): pl.pallas_call(ka, out_shape=[shape((2, 1536, GY), F32), shape((2, 1536,...  110 us
    pallas_call x1, Pallas kernels, on_device(): pl.pallas_call(kd, out_shape=shape((ROWS, COLS), F32), in_specs=[VM, VM,...  37.4 us
    pallas_call x1, Pallas kernels, on_device(): pl.pallas_call(k0, out_shape=shape((LT, NOBS, GY), F32), in_specs=[VM] *...  20.5 us

profile of v1, /device:TPU:225, one launch (start us, length us, event | category | flops | bytes accessed | tf_op | source)
XLA Modules:
  0.0 177.3 jit_solution(17069254043163451083)
XLA Ops:
  0.0 0.0 copy-start
  0.0 0.1 slice.30
  0.1 1.5 copy.13.obs_ref
  1.6 1.1 slice_multiply_fusion
  2.7 1.0 fusion
  3.7 0.1 concatenate.15
  3.8 0.9 slice_add_fusion.1
  4.8 1.3 broadcast_select_fusion
  6.1 0.7 stack.28
  6.9 0.0 copy-done
  6.9 0.7 stack.29
  7.6 0.9 pad.12.rows_ref
  8.5 0.9 pad.11.turned_ref
  9.4 20.5 %observe.1.t_ref = f32[4,256,128]{2,1,0:T(8,128)} custom-call(s32[1,256]{1,0:T(1,128)} %bitcast.39, f32[2048,512]{1,0:T(8,128)} %c_ref.5, f32[144,8,128]{2,1,0:T(8,128)} %pad.11.turned_ref), custom_call_target="tpu_custom_call" | custom-call | tf_op jit(solution)/shard_map/observe/pallas_call | solution.py:599
  29.8 110.1 %exchange.1 = (f32[2,1536,128]{2,1,0:T(8,128)}, f32[2,1536,128]{2,1,0:T(8,128)}, f32[4,512,128]{2,1,0:T(8,128)}, f32[4,512,128]{2,1,0:T(8,128)}, f32[4,256,128]{2,1,0:T(8,128)}, /*index=5*/f32[2,2,4,256,128]{4,3,2,1,0:T(8,128)}) custom-call(f32[2048,512]{1,0:T(8,128)} %c_ref.5, f32[4,256,128]{2,1,0:T(8,128)} %observe.1.t_ref, f32[144,8,128]{2,1,0:T(8,128)} %pad.12.rows_ref, ...), custom_call_target="tpu_custom_call" | custom-call | tf_op jit(solution)/shard_map/exchange/pallas_call | solution.py:612
  139.9 37.4 %update.1 = f32[2048,512]{1,0:T(8,128)} custom-call(f32[4,256,128]{2,1,0:T(8,128)} %get-tuple-element.11.pc_ref, f32[2,2,4,256,128]{4,3,2,1,0:T(8,128)} %get-tuple-element.12.pr_ref, f32[256,256]{1,0:T(8,128)} %f_ref.1, f32[144,8,128]{2,1,0:T(8,128)} %pad.12.rows_ref, f32[2048,512]{1,0:T(8,128)} %c_ref.5, f32[2,1536,128]{2,1,0:T(8,128)} %get-tuple-element.13.left_ref, ...), custom_call_target="tpu_custom_call" | custom-call | tf_op jit(solution)/shard_map/update/pallas_call | solution.py:644
  (6 shorter events, 0.1 us)
Async XLA Ops:
  0.0 6.9 %copy-start = (f32[16384]{0:T(1024)S(1)}, f32[16384]{0:T(1024)}, u32[]{:S(2)}) copy-start(f32[16384]{0:T(1024)} %param.9) | copy-start | bytes 196612

commit v2 on v1

v2 whole, which is shorter than its diff:
```python
import functools

import jax
import jax.numpy as jnp
from jax import lax
from jax.experimental import pallas as pl
from jax.experimental.pallas import tpu as pltpu
from jax.sharding import PartitionSpec as P

GX = 128
GY = 128
NOBS = 256
ROWS = 2048
COLS = 512
LT = 4
F32 = jnp.float32
BF = jnp.bfloat16
MESH = pl.DeviceIdType.MESH
PAD = 8
VM = pl.BlockSpec(memory_space=pltpu.VMEM)
ANY = pl.BlockSpec(memory_space=pl.ANY)


def split2(v):
    hi = v.astype(BF)
    return hi, (v - hi.astype(F32)).astype(BF)


def dot3(a, b, dims):
    (ah, al), (bh, bl) = split2(a), split2(b)
    dg = functools.partial(
        lax.dot_general, dimension_numbers=(dims, ((), ())), preferred_element_type=F32
    )
    return dg(ah, bh) + (dg(ah, bl) + dg(al, bh))


def fill_coefficients(k_ref, vel_ref, q_ref, cf):
    k, a, b = k_ref[...], vel_ref[0], vel_ref[1]
    lane = lax.broadcasted_iota(jnp.int32, (GX, GY), 1)
    east = jnp.where(lane < GY - 1, k - 0.5 * a, 0.0)
    west = jnp.where(lane > 0, k + 0.5 * a, 0.0)
    parts = [
        1.0 - 4.0 * k,
        k + 0.5 * b,
        k - 0.5 * b,
        east,
        west,
        q_ref[...],
        pltpu.roll(east, 1, 1),
        pltpu.roll(west, GY - 1, 1),
    ]
    for j, part in enumerate(parts):
        cf[j, 0:PAD] = jnp.zeros((PAD, GY), F32)
        cf[j, PAD : PAD + GX] = part
        cf[j, PAD + GX :] = jnp.zeros((PAD, GY), F32)


def spread_rows(cf, tile, first, count, out_ref):
    def body(g, _):
        for j in range(5):
            tile[j : j + 1, :] = cf[j, pl.ds(first + g, 1), :]
        turned = jnp.transpose(tile[...])
        for j in range(5):
            out_ref[j, pl.ds(pl.multiple_of(g * GY, GY), GY), :] = jnp.broadcast_to(
                turned[:, j : j + 1], (GY, GY)
            )
        return 0

    lax.fori_loop(0, count, body, 0)


def row_step(src, coef, base, lt, lead):
    at = pl.multiple_of(base + lead, 8)
    mid = src[lt, pl.ds(at, 8), :]
    north = src[lt, pl.ds(pl.multiple_of(at - GY, 8), 8), :]
    south = src[lt, pl.ds(pl.multiple_of(at + GY, 8), 8), :]
    east = src[lt, pl.ds(at + 1, 8), :]
    west = src[lt, pl.ds(at - 1, 8), :]
    return (coef[0] * mid + coef[1] * north) + (coef[2] * south + (coef[3] * east + coef[4] * west))


def col_two_steps(tiles, coef_ref, first):
    def step(v, g):
        c = [coef_ref[j, pl.ds(first + g, 1), :] for j in range(5)]
        east = pltpu.roll(v[g], GY - 1, 1)
        west = pltpu.roll(v[g], 1, 1)
        return (c[0] * v[g] + c[1] * v[g - 1]) + (c[2] * v[g + 1] + (c[3] * east + c[4] * west))

    v1 = {g: step(tiles, g) for g in range(-1, 5)}
    return [step(v1, g) for g in range(4)]


def observe(obs_ref, cf, oc, w, ext, t_ref, r):
    for h in range(2):
        ids = jnp.broadcast_to(obs_ref[:, GY * h : GY * (h + 1)].astype(F32), (8, GY))
        oc[GY * h : GY * (h + 1), :] = jnp.broadcast_to(
            jnp.transpose(ids)[:, 0:1], (GY, GY)
        ).astype(jnp.int32)
    lane = lax.broadcasted_iota(jnp.int32, (16, GY), 1)
    first = PAD + 16 * r

    def step(before, v, after, g):
        at = lambda j, n: cf[j, pl.ds(first + n, 1), :]
        east = pltpu.roll(v, GY - 1, 1)
        west = pltpu.roll(v, 1, 1)
        return (at(0, g) * v + at(2, g - 1) * before) + (
            at(1, g + 1) * after + (at(7, g) * east + at(6, g) * west)
        )

    def body(i, _):
        rows = pl.ds(pl.multiple_of(i * 16, 16), 16)
        ids = oc[rows, :] - lane
        e = {g: jnp.where(ids == (16 * r + g) * GY, 1.0, 0.0) for g in range(-2, 18)}
        u = {g: step(e[g - 1], e[g], e[g + 1], g) for g in range(-1, 17)}
        for g in range(16):
            w[rows, GY * g : GY * (g + 1)] = step(u[g - 1], u[g], u[g + 1], g)
        return 0

    lax.fori_loop(0, NOBS // 16, body, 0)
    for n in range(4):
        rows = pl.ds(512 * n, 512)
        block = jnp.concatenate([ext[2 + lt, rows, :] for lt in range(LT)], axis=1)
        t = dot3(w[:, 512 * n : 512 * (n + 1)], block, ((1,), (0,)))
        for lt in range(LT):
            part = t[:, lt * GY : (lt + 1) * GY]
            t_ref[lt] = part if n == 0 else t_ref[lt] + part


PIECES = ((0, 256), (1792, 256), (256, 512), (768, 512), (1280, 512))


def ka(
    c_ref,
    obs_ref,
    k_ref,
    vel_ref,
    q_ref,
    v_ref,
    halo_ref,
    spread_out,
    pc_ref,
    pr_ref,
    ext,
    v,
    spread,
    cf,
    tile,
    oc,
    w,
    t_ref,
    pc,
    pr,
    rs,
    zsum,
    zin,
    text,
    relay1,
    relay2,
    hsend,
    hrecv,
    send,
    recv,
    local,
):
    r = lax.axis_index("row")
    c = lax.axis_index("col")
    zh, x = r // 4, r % 4
    y, zl, k = c // 8, (c % 8) // 2, c % 2
    x_edge = jnp.where(zh == 0, 3, 0)
    has_left, has_right = c > 0, c < 31
    partner = (4 * (1 - zh) + x, c)
    x_peers = [(4 * zh + (x + d) % 4, c) for d in (1, 2, 3)]
    y_peers = [(r, 8 * ((y + d) % 4) + 2 * zl + k) for d in (1, 2, 3)]
    z_peers = [(r, 8 * y + 2 * ((zl + d) % 4) + k) for d in (1, 2, 3)]
    core = (r, c + 1 - 2 * k)
    x_to = 2 * (y - 2 * zh) + zl // 2
    gives = (y // 2 == zh) & jnp.logical_not((x_to == x) & (y == x))
    keeps = (y // 2 == zh) & (x_to == x) & (y == x)
    give_to = (4 * zh + jnp.where(gives, x_to, x), 8 * x + 2 * zl + k)
    y_from = 2 * zh + x // 2
    pair = x % 2
    holder = zl // 2 == pair
    near = zl == 2 - pair
    s = zl % 2
    near_z = (r, 8 * y + 2 * (2 - pair) + k)
    far_z = (r, 8 * y + 6 * (1 - pair) + k)
    twin_z = (r, 8 * y + 2 * (zl + 1 - 2 * s) + k)
    takes = holder & jnp.logical_not((y_from == y) & (x == y))
    take_from = (4 * zh + y, 8 * y_from + 2 * zl + k)

    def remote(src, dst, s, t, device):
        return pltpu.make_async_remote_copy(
            src_ref=src,
            dst_ref=dst,
            send_sem=send.at[s],
            recv_sem=recv.at[t],
            device_id=device,
            device_id_type=MESH,
        )

    barrier = pltpu.get_barrier_semaphore()

    def greet(device):
        pl.semaphore_signal(barrier, inc=1, device_id=device, device_id_type=MESH)

    for device in x_peers + y_peers + z_peers + [partner, core]:
        greet(device)
    left, right = (r, jnp.maximum(c - 1, 0)), (r, jnp.minimum(c + 1, 31))
    pl.when(has_left)(lambda: greet(left))
    pl.when(has_right)(lambda: greet(right))
    pl.when(gives)(lambda: greet(give_to))
    pl.when(takes)(lambda: greet(take_from))
    one = lambda flag: jnp.where(flag, 1, 0)
    pl.semaphore_wait(
        barrier, 11 + one(has_left) + one(has_right) + one(gives) + one(takes)
    )

    def halo_out(side, piece, t):
        start, rows = PIECES[piece]
        src = c_ref.at[pl.ds(start, rows), pl.ds(GY * t + (256 if side == 1 else 0), GY)]
        dst = ext.at[t + (0 if side == 1 else 6), pl.ds(start, rows)]
        sem = side * 10 + piece * 2 + t
        return pltpu.make_async_remote_copy(
            src_ref=src,
            dst_ref=dst,
            send_sem=hsend.at[sem],
            recv_sem=hrecv.at[sem],
            device_id=right if side == 1 else left,
            device_id_type=MESH,
        )

    flags = {0: (has_left, has_right), 1: (has_right, has_left)}

    def halo_start(piece):
        for side in (0, 1):

            @pl.when(flags[side][0])
            def _():
                for t in (0, 1):
                    halo_out(side, piece, t).start()

    def halo_arrive(piece):
        for side in (0, 1):

            @pl.when(flags[side][1])
            def _():
                for t in (0, 1):
                    halo_out(side, piece, t).wait_recv()

    first = PAD + 4 * c

    def transport(piece):
        halo_arrive(piece)
        start, rows = PIECES[piece]

        def body(i, _):
            at = pl.ds(pl.multiple_of(start + i * 16, 16), 16)
            out = col_two_steps({g - 2: ext[g, at, :] for g in range(8)}, cf, first)
            for lt in range(LT):
                v[lt, at, :] = out[lt]
            return 0

        lax.fori_loop(0, rows // 16, body, 0, unroll=2)
        copy = pltpu.make_async_copy(
            v.at[:, pl.ds(start, rows)], v_ref.at[:, pl.ds(start, rows)], local.at[4 + piece]
        )
        copy.start()
        return copy

    halo_start(0)
    halo_start(1)
    inner = [
        pltpu.make_async_copy(c_ref.at[:, pl.ds(GY * t, GY)], ext.at[2 + t], local.at[t])
        for t in range(LT)
    ]
    for copy in inner:
        copy.start()
    halo_start(2)
    for side, tiles in ((0, (6, 7)), (1, (0, 1))):

        @pl.when(jnp.logical_not(flags[side][1]))
        def _():
            for t in tiles:
                ext[t] = jnp.zeros((ROWS, GY), F32)

    fill_coefficients(k_ref, vel_ref, q_ref, cf)
    for copy in inner:
        copy.wait()
    observe(obs_ref, cf, oc, w, ext, t_ref, r)

    def rs_copy(d):
        there = (x + d + 1) % 4
        return remote(
            t_ref.at[:, pl.ds(pl.multiple_of(64 * there, 64), 64), :],
            rs.at[d],
            12 + d,
            12 + d,
            x_peers[d],
        )

    for d in range(3):
        rs_copy(d).start()
    halo_start(3)

    v_out = [transport(0), transport(1)]

    top, bottom = pl.ds(0, 256), pl.ds(1792, 256)
    above, below = pl.ds(0, 256), pl.ds(256, 256)
    up_near, down_near = x > 0, x < 3
    up_to = (4 * zh + jnp.maximum(x - 1, 0), c)
    down_to = (4 * zh + jnp.minimum(x + 1, 3), c)
    up_copy = remote(v.at[:, top], halo_ref.at[:, below], 16, 16, up_to)
    down_copy = remote(v.at[:, bottom], halo_ref.at[:, above], 17, 17, down_to)
    pl.when(up_near)(lambda: up_copy.start())
    pl.when(down_near)(lambda: down_copy.start())
    at_edge = x == x_edge
    far = (4 * zh + x_edge, c)
    cross = pl.ds(pl.multiple_of(jnp.where(zh == 0, 1792, 0), 256), 256)
    hop1 = [
        (j, remote(v.at[j, cross], relay1, 18 + j, 18, (4 * zh + j, c))) for j in range(4)
    ]
    keep1 = pltpu.make_async_copy(v.at[x, cross], relay1, local.at[9])

    @pl.when(at_edge)
    def _():
        for j, copy in hop1:
            pl.when(x != j)(lambda copy=copy: copy.start())
        keep1.start()

    for d in range(3):
        rs_copy(d).wait()
    mine = pl.ds(pl.multiple_of(64 * x, 64), 64)
    for lt in range(LT):
        zsum[lt] = (t_ref[lt, mine, :] + rs[0, lt]) + (rs[1, lt] + rs[2, lt])
    z_copy = remote(zsum, zin, 15, 15, partner)
    z_copy.start()

    spread_rows(cf, tile, PAD + 16 * r - 1, 18, spread)
    spread_copy = pltpu.make_async_copy(spread, spread_out, local.at[14])
    spread_copy.start()

    hop2 = remote(relay1, relay2, 24, 24, partner)
    pl.when(at_edge)(lambda: keep1.wait())
    pl.when(jnp.logical_not(at_edge))(lambda: hop1[0][1].wait_recv())
    hop2.start()

    z_copy.wait()
    for lt in range(LT):
        text[2 + lt] = zsum[lt] + zin[lt]
    t_right = remote(text.at[pl.ds(4, 2)], text.at[pl.ds(0, 2)], 22, 22, right)
    t_left = remote(text.at[pl.ds(2, 2)], text.at[pl.ds(6, 2)], 23, 23, left)
    pl.when(has_right)(lambda: t_right.start())
    pl.when(has_left)(lambda: t_left.start())
    halo_start(4)
    for there, copy, tiles in ((has_left, t_right, (0, 1)), (has_right, t_left, (6, 7))):
        pl.when(there)(lambda copy=copy: copy.wait_recv())

        @pl.when(jnp.logical_not(there))
        def _():
            for t in tiles:
                text[t] = jnp.zeros((64, GY), F32)

    for h in range(4):
        at = pl.ds(16 * h, 16)
        out = col_two_steps({g - 2: text[g, at, :] for g in range(8)}, cf, first)
        for lt in range(LT):
            ids = c * COLS + lt * GY + lax.broadcasted_iota(jnp.int32, (16, GY), 1)
            noise = jnp.broadcast_to(cf[5, pl.ds(first + lt, 1), :], (16, GY))
            my_obs = oc[pl.ds(pl.multiple_of(64 * x + 16 * h, 16), 16), :]
            zsum[lt, at, :] = out[lt] + jnp.where(my_obs == ids, noise, 0.0)
    p_copy = [remote(zsum, pc.at[:, mine], 25 + d, 25 + d, x_peers[d]) for d in range(3)]
    mine_y = pl.ds(pl.multiple_of(64 * y, 64), 64)
    a_copy = remote(zsum, pr.at[k, s, :, mine], 28, 28, give_to)
    a_keep = pltpu.make_async_copy(zsum, pr.at[k, s, :, mine], local.at[10])
    pl.when(gives)(lambda: a_copy.start())
    pl.when(keeps)(lambda: a_keep.start())
    for copy in p_copy:
        copy.start()
    for lt in range(LT):
        pc[lt, mine, :] = zsum[lt]

    piece = pr.at[k, s, :, mine_y]
    slab = pr.at[k, :, :, mine_y]
    b_twin = remote(piece, piece, 29, 29 + s, twin_z)
    b_near = remote(piece, piece, 30, 29 + s, near_z)
    b_far = remote(slab, slab, 31, 31, far_z)
    a_wait = remote(zsum, piece, 28, 28, give_to)

    @pl.when(holder)
    def _():
        pl.when(takes)(lambda: a_wait.wait_recv())
        pl.when(jnp.logical_not(takes))(lambda: a_keep.wait())
        b_near.start()
        b_twin.start()

    v_out.append(transport(2))
    for t in range(2):
        other = pr.at[k, t, :, mine_y]
        arrive = remote(other, other, 29, 29 + t, twin_z)
        pl.when(near | (holder & (s != t)))(lambda arrive=arrive: arrive.wait_recv())
    pl.when(near)(lambda: b_far.start())
    pl.when(jnp.logical_not(near | holder))(lambda: b_far.wait_recv())

    hop3 = remote(relay2, halo_ref.at[x, into2(zh)], 38, 38 + 0, far)
    hop2.wait_recv()
    last = pltpu.make_async_copy(relay2, halo_ref.at[x, into2(zh)], local.at[11])
    pl.when(at_edge)(lambda: last.start())

    def forward(j):
        return remote(relay2, halo_ref.at[j, into2(zh)], 38, 38 + j, far)

    for j in range(4):

        @pl.when(jnp.logical_not(at_edge) & (x == j))
        def _():
            forward(j).start()

    c_copy = [remote(slab, slab, 32 + d, 32 + d, y_peers[d]) for d in range(3)]
    for copy in c_copy:
        copy.start()
    v_out.append(transport(3))
    for d in range(3):
        there = pl.ds(pl.multiple_of(64 * ((y + 3 - d) % 4), 64), 64)
        slab_in = pr.at[k, :, :, there]
        remote(slab_in, slab_in, 32 + d, 32 + d, y_peers[d]).wait_recv()
    d_copy = remote(pr.at[k], pr.at[k], 35, 35, core)
    d_copy.start()
    for copy in p_copy:
        copy.wait_recv()
    pc_out = pltpu.make_async_copy(pc, pc_ref, local.at[12])
    pc_out.start()
    other = pr.at[1 - k]
    remote(other, other, 35, 35, core).wait_recv()
    pr_out = pltpu.make_async_copy(pr, pr_ref, local.at[13])
    pr_out.start()

    v_out.append(transport(4))

    for copy in v_out:
        copy.wait()
    spread_copy.wait()
    pl.when(up_near)(lambda: up_copy.wait_send())
    pl.when(down_near)(lambda: down_copy.wait_send())
    pl.when(down_near)(lambda: up_copy.wait_recv())
    pl.when(up_near)(lambda: down_copy.wait_recv())

    @pl.when(at_edge)
    def _():
        for j, copy in hop1:
            pl.when(x != j)(lambda copy=copy: copy.wait_send())
        last.wait()
        for j in range(4):
            pl.when(x != j)(lambda j=j: forward(j).wait_recv())

    hop2.wait_send()
    pl.when(jnp.logical_not(at_edge))(lambda: hop3.wait_send())
    pl.when(has_right)(lambda: t_right.wait_send())
    pl.when(has_left)(lambda: t_left.wait_send())
    for copy in p_copy:
        copy.wait_send()
    pl.when(gives)(lambda: a_copy.wait_send())

    @pl.when(holder)
    def _():
        b_near.wait_send()
        b_twin.wait_send()

    pl.when(near)(lambda: b_far.wait_send())
    for copy in c_copy + [d_copy]:
        copy.wait_send()
    for side in (0, 1):

        @pl.when(flags[side][0])
        def _():
            for piece in range(5):
                for t in (0, 1):
                    halo_out(side, piece, t).wait_send()

    pc_out.wait()
    pr_out.wait()


def into2(zh):
    return pl.ds(pl.multiple_of(jnp.where(zh == 0, 256, 0), 256), 256)


def kd(pc_ref, pr_ref, f_ref, q_ref, v_in, halo_ref, spread_in, o_ref, v, v1, spread, out, sem, osem):
    r = lax.axis_index("row")
    c = lax.axis_index("col")
    copies = [
        pltpu.make_async_copy(v_in, v.at[:, pl.ds(256, ROWS)], sem.at[0]),
        pltpu.make_async_copy(spread_in, spread, sem.at[1]),
    ]
    for copy in copies:
        copy.start()
    guarded = [
        (r > 0, halo_ref.at[:, pl.ds(0, 256)], v.at[:, pl.ds(0, 256)], sem.at[2]),
        (r < 7, halo_ref.at[:, pl.ds(256, 256)], v.at[:, pl.ds(2304, 256)], sem.at[3]),
    ]
    for flag, src, dst, s in guarded:

        @pl.when(flag)
        def _():
            pltpu.make_async_copy(src, dst, s).start()

        @pl.when(jnp.logical_not(flag))
        def _():
            dst[...] = jnp.zeros(dst.shape, F32)

    f = f_ref[...]
    g = dot3(f, f, ((0,), (0,)))
    pc = jnp.concatenate([pc_ref[lt] for lt in range(LT)], axis=1)
    w = dot3(g, pc, ((1,), (0,)))
    for ci in range(4):
        lhs = jnp.concatenate([pr_ref[ci % 2, ci // 2, lt] for lt in range(LT)], axis=1)
        u = dot3(lhs, w, ((0,), (0,)))
        for lt in range(LT):
            out[lt, pl.ds(512 * ci, 512), :] = u[:, lt * GY : (lt + 1) * GY]

    for copy in copies:
        copy.wait()
    for flag, src, dst, s in guarded:

        @pl.when(flag)
        def _():
            pltpu.make_async_copy(src, dst, s).wait()

    def one(i, _):
        base = pl.multiple_of(i * 8, 8)
        coef = [spread[j, pl.ds(base, 8), :] for j in range(5)]
        for lt in range(LT):
            v1[lt, pl.ds(base, 8), :] = row_step(v, coef, base, lt, GY)
        return 0

    lax.fori_loop(0, 2304 // 8, one, 0, unroll=4)

    def store(n):
        return [
            pltpu.make_async_copy(
                out.at[lt, pl.ds(pl.multiple_of(n * 256, 256), 256)],
                o_ref.at[pl.ds(pl.multiple_of(n * 256, 256), 256), pl.ds(GY * lt, GY)],
                osem.at[n, lt],
            )
            for lt in range(LT)
        ]

    def block(n, _):
        def two(i, _):
            base = pl.multiple_of(n * 256 + i * 8, 8)
            coef = [spread[j, pl.ds(pl.multiple_of(base + GY, 8), 8), :] for j in range(5)]
            for lt in range(LT):
                at = pl.ds(base, 8)
                out[lt, at, :] = row_step(v1, coef, base, lt, GY) - out[lt, at, :]
            return 0

        lax.fori_loop(0, 256 // 8, two, 0, unroll=4)

        @pl.when((c // 4 == r) & (n // 2 == c % 4))
        def _():
            i0 = lax.broadcasted_iota(jnp.int32, (GY, GY), 0)
            i1 = lax.broadcasted_iota(jnp.int32, (GY, GY), 1)
            for h in range(2):
                lt = 2 * (n % 2) + h
                at = pl.ds(pl.multiple_of(n * 256 + h * GY, GY), GY)
                noise = jnp.broadcast_to(q_ref[pl.ds(4 * c + lt, 1), :], (GY, GY))
                out[lt, at, :] = out[lt, at, :] + jnp.where(i0 == i1, noise, 0.0)

        for copy in store(n):
            copy.start()
        return 0

    lax.fori_loop(0, ROWS // 256, block, 0)
    for n in range(ROWS // 256):
        for copy in store(n):
            copy.wait()


def on_device(prior_cov, diffusivity, velocity, variance, observed_index, innov_factor):
    shape = jax.ShapeDtypeStruct
    limit = 60 * 1024 * 1024
    k = diffusivity.reshape(GX, GY)
    vel = velocity.reshape(2, GX, GY)
    q = variance.reshape(GX, GY)
    v, halo, spread, pc, pr = pl.pallas_call(
        ka,
        out_shape=[
            shape((LT, ROWS, GY), F32),
            shape((LT, 512, GY), F32),
            shape((5, 2304, GY), F32),
            shape((LT, NOBS, GY), F32),
            shape((2, 2, LT, NOBS, GY), F32),
        ],
        in_specs=[ANY, VM, VM, VM, VM],
        out_specs=[ANY] * 5,
        scratch_shapes=[
            pltpu.VMEM((8, ROWS, GY), F32),
            pltpu.VMEM((LT, ROWS, GY), F32),
            pltpu.VMEM((5, 2304, GY), F32),
            pltpu.VMEM((8, GX + 2 * PAD, GY), F32),
            pltpu.VMEM((8, GY), F32),
            pltpu.VMEM((NOBS, GY), jnp.int32),
            pltpu.VMEM((NOBS, ROWS), F32),
            pltpu.VMEM((LT, NOBS, GY), F32),
            pltpu.VMEM((LT, NOBS, GY), F32),
            pltpu.VMEM((2, 2, LT, NOBS, GY), F32),
            pltpu.VMEM((3, LT, 64, GY), F32),
            pltpu.VMEM((LT, 64, GY), F32),
            pltpu.VMEM((LT, 64, GY), F32),
            pltpu.VMEM((8, 64, GY), F32),
            pltpu.VMEM((256, GY), F32),
            pltpu.VMEM((256, GY), F32),
            pltpu.SemaphoreType.DMA((20,)),
            pltpu.SemaphoreType.DMA((20,)),
            pltpu.SemaphoreType.DMA((40,)),
            pltpu.SemaphoreType.DMA((42,)),
            pltpu.SemaphoreType.DMA((15,)),
        ],
        compiler_params=pltpu.CompilerParams(
            collective_id=0, has_side_effects=True, vmem_limit_bytes=limit
        ),
        name="exchange",
    )(prior_cov, observed_index.reshape(1, NOBS), k, vel, q)
    return pl.pallas_call(
        kd,
        out_shape=shape((ROWS, COLS), F32),
        in_specs=[VM] * 4 + [ANY] * 3,
        out_specs=ANY,
        scratch_shapes=[
            pltpu.VMEM((LT, 2560, GY), F32),
            pltpu.VMEM((LT, 2304, GY), F32),
            pltpu.VMEM((5, 2304, GY), F32),
            pltpu.VMEM((LT, ROWS, GY), F32),
            pltpu.SemaphoreType.DMA((4,)),
            pltpu.SemaphoreType.DMA((ROWS // 256, LT)),
        ],
        compiler_params=pltpu.CompilerParams(vmem_limit_bytes=limit),
        name="update",
    )(pc, pr, innov_factor, q, v, halo, spread)


def solution(mesh):
    return jax.shard_map(
        on_device,
        mesh=mesh,
        in_specs=(P("row", "col"), P(), P(), P(), P(), P()),
        out_specs=P("row", "col"),
        check_vma=False,
    )
```

time: 178 us -> 117 us (0.66)
  the two profiles are of different devices: /device:TPU:225 before, /device:TPU:97 now
where the time goes in v2:
time: 117 us
  Pallas kernels  115 us (98%)
  local copies, waits for them, and re-layouts  1.57 us (1%)
    pallas_call x1, Pallas kernels, on_device(): pl.pallas_call(ka, out_shape=[shape((LT, ROWS, GY), F32), shape((LT, 512,...  103 us
    pallas_call x1, Pallas kernels, on_device(): pl.pallas_call(kd, out_shape=shape((ROWS, COLS), F32), in_specs=[VM] * 4...  12.3 us

profile of v2, /device:TPU:97, one launch (start us, length us, event | category | flops | bytes accessed | tf_op | source)
XLA Modules:
  0.0 116.6 jit_solution(18438273087749510578)
XLA Ops:
  0.0 1.6 %copy.9 = f32[1,2,128,128]{3,2,1,0:T(8,128)} copy(f32[1,2,128,128]{3,1,2,0:T(2,128)} %bitcast.10) | data formatting | bytes 262144
  1.6 102.7 %exchange.1 = (f32[4,2048,128]{2,1,0:T(8,128)}, f32[4,512,128]{2,1,0:T(8,128)}, f32[5,2304,128]{2,1,0:T(8,128)}, f32[4,256,128]{2,1,0:T(8,128)}, f32[2,2,4,256,128]{4,3,2,1,0:T(8,128)}) custom-call(f32[2048,512]{1,0:T(8,128)} %c_ref.1, s32[1,256]{1,0:T(1,128)} %bitcast.12, f32[128,128]{1,0:T(8,128)} %bitcast.11, f32[2,128,128]{2,1,0:T(8,128)} %bitcast.7, ...), custom_call_target="tpu_custom_call" | custom-call | tf_op jit(solution)/shard_map/exchange/pallas_call | solution.py:584
  104.3 12.3 %update.1 = f32[2048,512]{1,0:T(8,128)} custom-call(f32[4,256,128]{2,1,0:T(8,128)} %get-tuple-element.10.pc_ref, f32[2,2,4,256,128]{4,3,2,1,0:T(8,128)} %get-tuple-element.11.pr_ref, f32[256,256]{1,0:T(8,128)} %f_ref.1, f32[128,128]{1,0:T(8,128)} %bitcast.9, f32[4,2048,128]{2,1,0:T(8,128)} %get-tuple-element.12.v_in, ...), custom_call_target="tpu_custom_call" | custom-call | tf_op jit(solution)/shard_map/update/pallas_call | solution.py:623

commit v3 on v2

v3 whole, which is shorter than its diff:
```python
import functools

import jax
import jax.numpy as jnp
from jax import lax
from jax.experimental import pallas as pl
from jax.experimental.pallas import tpu as pltpu
from jax.sharding import PartitionSpec as P

GX = 128
GY = 128
NOBS = 256
ROWS = 2048
COLS = 512
LT = 4
F32 = jnp.float32
BF = jnp.bfloat16
MESH = pl.DeviceIdType.MESH
PAD = 8
VM = pl.BlockSpec(memory_space=pltpu.VMEM)
ANY = pl.BlockSpec(memory_space=pl.ANY)


def split2(v):
    hi = v.astype(BF)
    return hi, (v - hi.astype(F32)).astype(BF)


def dot3(a, b, dims):
    (ah, al), (bh, bl) = split2(a), split2(b)
    dg = functools.partial(
        lax.dot_general, dimension_numbers=(dims, ((), ())), preferred_element_type=F32
    )
    return dg(ah, bh) + (dg(ah, bl) + dg(al, bh))


def fill_coefficients(k_ref, vel_ref, q_ref, speed, cf):
    for j in range(2):
        for g in range(GX):
            speed[j, g : g + 1, :] = vel_ref[j : j + 1, GY * g : GY * (g + 1)]
    k, a, b = k_ref[...], speed[0], speed[1]
    lane = lax.broadcasted_iota(jnp.int32, (GX, GY), 1)
    east = jnp.where(lane < GY - 1, k - 0.5 * a, 0.0)
    west = jnp.where(lane > 0, k + 0.5 * a, 0.0)
    parts = [
        1.0 - 4.0 * k,
        k + 0.5 * b,
        k - 0.5 * b,
        east,
        west,
        q_ref[...],
        pltpu.roll(east, 1, 1),
        pltpu.roll(west, GY - 1, 1),
    ]
    for j, part in enumerate(parts):
        cf[j, 0:PAD] = jnp.zeros((PAD, GY), F32)
        cf[j, PAD : PAD + GX] = part
        cf[j, PAD + GX :] = jnp.zeros((PAD, GY), F32)


def spread_rows(cf, tile, first, count, out_ref):
    def body(g, _):
        for j in range(5):
            tile[j : j + 1, :] = cf[j, pl.ds(first + g, 1), :]
        turned = jnp.transpose(tile[...])
        for j in range(5):
            out_ref[j, pl.ds(pl.multiple_of(g * GY, GY), GY), :] = jnp.broadcast_to(
                turned[:, j : j + 1], (GY, GY)
            )
        return 0

    lax.fori_loop(0, count, body, 0)


def row_step(src, coef, base, lt, lead):
    at = pl.multiple_of(base + lead, 8)
    mid = src[lt, pl.ds(at, 8), :]
    north = src[lt, pl.ds(pl.multiple_of(at - GY, 8), 8), :]
    south = src[lt, pl.ds(pl.multiple_of(at + GY, 8), 8), :]
    east = src[lt, pl.ds(at + 1, 8), :]
    west = src[lt, pl.ds(at - 1, 8), :]
    return (coef[0] * mid + coef[1] * north) + (coef[2] * south + (coef[3] * east + coef[4] * west))


def col_two_steps(tiles, coef_ref, first):
    def step(v, g):
        c = [coef_ref[j, pl.ds(first + g, 1), :] for j in range(5)]
        east = pltpu.roll(v[g], GY - 1, 1)
        west = pltpu.roll(v[g], 1, 1)
        return (c[0] * v[g] + c[1] * v[g - 1]) + (c[2] * v[g + 1] + (c[3] * east + c[4] * west))

    v1 = {g: step(tiles, g) for g in range(-1, 5)}
    return [step(v1, g) for g in range(4)]


def observe(obs_ref, cf, oc, w, ext, t_ref, r):
    for h in range(2):
        ids = jnp.broadcast_to(obs_ref[:, GY * h : GY * (h + 1)].astype(F32), (8, GY))
        oc[GY * h : GY * (h + 1), :] = jnp.broadcast_to(
            jnp.transpose(ids)[:, 0:1], (GY, GY)
        ).astype(jnp.int32)
    lane = lax.broadcasted_iota(jnp.int32, (32, GY), 1)
    first = PAD + 16 * r

    def step(before, v, after, g):
        at = lambda j, n: cf[j, pl.ds(first + n, 1), :]
        east = pltpu.roll(v, GY - 1, 1)
        west = pltpu.roll(v, 1, 1)
        return (at(0, g) * v + at(2, g - 1) * before) + (
            at(1, g + 1) * after + (at(7, g) * east + at(6, g) * west)
        )

    def body(i, _):
        rows = pl.ds(pl.multiple_of(i * 32, 32), 32)
        ids = oc[rows, :] - lane
        e = {g: jnp.where(ids == (16 * r + g) * GY, 1.0, 0.0) for g in range(-2, 18)}
        u = {g: step(e[g - 1], e[g], e[g + 1], g) for g in range(-1, 17)}
        for g in range(16):
            w[rows, GY * g : GY * (g + 1)] = step(u[g - 1], u[g], u[g + 1], g)
        return 0

    lax.fori_loop(0, NOBS // 32, body, 0)
    for n in range(4):
        rows = pl.ds(512 * n, 512)
        block = jnp.concatenate([ext[2 + lt, rows, :] for lt in range(LT)], axis=1)
        t = dot3(w[:, 512 * n : 512 * (n + 1)], block, ((1,), (0,)))
        for lt in range(LT):
            part = t[:, lt * GY : (lt + 1) * GY]
            t_ref[lt] = part if n == 0 else t_ref[lt] + part


PIECES = (0, 1792, 256, 512, 768, 1024, 1280, 1536)


def ka(
    c_ref,
    obs_ref,
    k_ref,
    vel_ref,
    q_ref,
    f_ref,
    p_ref,
    ext,
    v,
    v1,
    out,
    spread,
    cf,
    speed,
    tile,
    oc,
    w,
    t_ref,
    pc,
    pr,
    rs,
    psum,
    zin,
    text,
    relay1,
    relay2,
    hsend,
    hrecv,
    send,
    recv,
    local,
):
    r = lax.axis_index("row")
    c = lax.axis_index("col")
    zh, x = r // 4, r % 4
    y, zl, k = c // 8, (c % 8) // 2, c % 2
    no = jnp.logical_not
    x_edge = jnp.where(zh == 0, 3, 0)
    has_left, has_right = c > 0, c < 31
    c_left, c_right = jnp.maximum(c - 1, 0), jnp.minimum(c + 1, 31)
    r_far = 4 * (1 - zh) + x
    left, right, partner = (r, c_left), (r, c_right), (r_far, c)
    left_far, right_far = (r_far, c_left), (r_far, c_right)
    x_peers = [(4 * zh + (x + d) % 4, c) for d in (1, 2, 3)]
    y_peers = [(r, 8 * ((y + d) % 4) + 2 * zl + k) for d in (1, 2, 3)]
    z_peers = [(r, 8 * y + 2 * ((zl + d) % 4) + k) for d in (1, 2, 3)]
    core = (r, c + 1 - 2 * k)
    x_to = 2 * (y - 2 * zh) + zl // 2
    keeps = (y // 2 == zh) & (x_to == x) & (y == x)
    gives = (y // 2 == zh) & no(keeps)
    give_to = (4 * zh + jnp.where(gives, x_to, x), 8 * x + 2 * zl + k)
    y_from = 2 * zh + x // 2
    pair = x % 2
    holder = zl // 2 == pair
    near = zl == 2 - pair
    far = no(holder | near)
    takes = holder & no((y_from == y) & (x == y))
    take_from = (4 * zh + y, 8 * y_from + 2 * zl + k)
    s = zl % 2
    near_z = (r, 8 * y + 2 * (2 - pair) + k)
    far_z = (r, 8 * y + 6 * (1 - pair) + k)
    twin_z = (r, 8 * y + 2 * (zl + 1 - 2 * s) + k)

    def remote(src, dst, i, j, device, h=0):
        return pltpu.make_async_remote_copy(
            src_ref=src,
            dst_ref=dst,
            send_sem=send.at[h, i],
            recv_sem=recv.at[h, j],
            device_id=device,
            device_id_type=MESH,
        )

    halves = range(2)

    def rows_of(h, n):
        return pl.ds(pl.multiple_of(128 * h + 32 * n, 32), 32)

    barrier = pltpu.get_barrier_semaphore()

    def greet(*devices):
        for device in devices:
            pl.semaphore_signal(barrier, inc=1, device_id=device, device_id_type=MESH)

    greet(*x_peers, *y_peers, *z_peers, partner, core)
    pl.when(has_left)(lambda: greet(left, left_far))
    pl.when(has_right)(lambda: greet(right, right_far))
    pl.when(gives)(lambda: greet(give_to))
    pl.when(takes)(lambda: greet(take_from))
    one = lambda flag: jnp.where(flag, 1, 0)
    pl.semaphore_wait(
        barrier, 11 + 2 * one(has_left) + 2 * one(has_right) + one(gives) + one(takes)
    )

    def halo_out(side, piece, t):
        rows = pl.ds(PIECES[piece], 256)
        sem = side * 16 + piece * 2 + t
        return pltpu.make_async_remote_copy(
            src_ref=c_ref.at[rows, pl.ds(GY * t + (256 if side == 1 else 0), GY)],
            dst_ref=ext.at[t + (0 if side == 1 else 6), rows],
            send_sem=hsend.at[sem],
            recv_sem=hrecv.at[sem],
            device_id=right if side == 1 else left,
            device_id_type=MESH,
        )

    flags = {0: (has_left, has_right), 1: (has_right, has_left)}

    def halo_start(piece):
        for side in (0, 1):

            @pl.when(flags[side][0])
            def _():
                for t in (0, 1):
                    halo_out(side, piece, t).start()

    first = PAD + 4 * c

    def transport(piece):
        for side in (0, 1):

            @pl.when(flags[side][1])
            def _():
                for t in (0, 1):
                    halo_out(side, piece, t).wait_recv()

        def body(i, _):
            at = pl.ds(pl.multiple_of(PIECES[piece] + i * 16, 16), 16)
            to = pl.ds(pl.multiple_of(PIECES[piece] + 256 + i * 16, 16), 16)
            res = col_two_steps({g - 2: ext[g, at, :] for g in range(8)}, cf, first)
            for lt in range(LT):
                v[lt, to, :] = res[lt]
            return 0

        lax.fori_loop(0, 256 // 16, body, 0, unroll=2)

    def along_rows(one, two):
        def step_one(i, _):
            base = pl.multiple_of(i * 8, 8)
            coef = [spread[j, pl.ds(base, 8), :] for j in range(5)]
            for lt in range(LT):
                v1[lt, pl.ds(base, 8), :] = row_step(v, coef, base, lt, GY)
            return 0

        def step_two(i, _):
            base = pl.multiple_of(i * 8, 8)
            at = pl.ds(base, 8)
            coef = [spread[j, pl.ds(pl.multiple_of(base + GY, 8), 8), :] for j in range(5)]
            for lt in range(LT):
                out[lt, at, :] = out[lt, at, :] + row_step(v1, coef, base, lt, GY)
            return 0

        if one:
            lax.fori_loop((one[0] + 1) * 16, (one[1] + 1) * 16, step_one, 0, unroll=4)
        if two:
            lax.fori_loop(two[0] * 16, two[1] * 16, step_two, 0, unroll=4)

    def begin_out():
        def clear(i, _):
            for lt in range(LT):
                out[lt, pl.ds(pl.multiple_of(i * 64, 64), 64), :] = jnp.zeros((64, GY), F32)
            return 0

        lax.fori_loop(0, ROWS // 64, clear, 0)

        @pl.when(c // 4 == r)
        def _():
            i0 = lax.broadcasted_iota(jnp.int32, (GY, GY), 0)
            i1 = lax.broadcasted_iota(jnp.int32, (GY, GY), 1)
            for lt in range(LT):
                at = pl.ds(pl.multiple_of(512 * (c % 4) + GY * lt, GY), GY)
                noise = jnp.broadcast_to(cf[5, pl.ds(first + lt, 1), :], (GY, GY))
                out[lt, at, :] = jnp.where(i0 == i1, noise, 0.0)

    def subtract(kk, s_, weights):
        ci = 2 * s_ + kk
        lhs = jnp.concatenate([pr[kk, s_, lt] for lt in range(LT)], axis=1)
        u = dot3(lhs, weights, ((0,), (0,)))
        at = pl.ds(pl.multiple_of(512 * ci, 512), 512)
        for lt in range(LT):
            out[lt, at, :] = out[lt, at, :] - u[:, lt * GY : (lt + 1) * GY]

    halo_start(0)
    halo_start(1)
    inner = [
        pltpu.make_async_copy(c_ref.at[:, pl.ds(GY * t, GY)], ext.at[2 + t], local.at[t])
        for t in range(LT)
    ]
    for copy in inner:
        copy.start()
    halo_start(2)
    fill_coefficients(k_ref, vel_ref, q_ref, speed, cf)
    for copy in inner:
        copy.wait()
    observe(obs_ref, cf, oc, w, ext, t_ref, r)

    def rs_copy(h, d):
        there = rows_of(h, (x + d + 1) % 4)
        return remote(t_ref.at[:, there, :], rs.at[h, d], 12 + d, 12 + d, x_peers[d], h)

    for h in halves:
        for d in range(3):
            rs_copy(h, d).start()
    halo_start(3)
    for side, tiles in ((0, (6, 7)), (1, (0, 1))):

        @pl.when(no(flags[side][1]))
        def _():
            for t in tiles:
                ext[t] = jnp.zeros((ROWS, GY), F32)
                for h in halves:
                    text[h, t] = jnp.zeros((32, GY), F32)
                    zin[h, t] = jnp.zeros((32, GY), F32)

    transport(0)
    transport(1)
    top, bottom = pl.ds(256, 256), pl.ds(2048, 256)
    above, below = pl.ds(0, 256), pl.ds(2304, 256)
    up_near, down_near = x > 0, x < 3
    up_to = (4 * zh + jnp.maximum(x - 1, 0), c)
    down_to = (4 * zh + jnp.minimum(x + 1, 3), c)
    up_copy = remote(v.at[:, top], v.at[:, below], 16, 16, up_to)
    down_copy = remote(v.at[:, bottom], v.at[:, above], 17, 17, down_to)
    pl.when(up_near)(lambda: up_copy.start())
    pl.when(down_near)(lambda: down_copy.start())
    at_edge = x == x_edge
    edge = (4 * zh + x_edge, c)
    cross = pl.ds(pl.multiple_of(jnp.where(zh == 0, 2048, 256), 256), 256)
    into = pl.ds(pl.multiple_of(jnp.where(zh == 0, 2304, 0), 256), 256)
    hop1 = [remote(v.at[j, cross], relay1, 18 + j, 18, (4 * zh + j, c)) for j in range(4)]
    keep1 = pltpu.make_async_copy(v.at[x, cross], relay1, local.at[4])

    @pl.when(at_edge)
    def _():
        for j, copy in enumerate(hop1):
            pl.when(x != j)(lambda copy=copy: copy.start())
        keep1.start()

    whole, low, high = pl.ds(2, 4), pl.ds(2, 2), pl.ds(4, 2)
    before, after = pl.ds(0, 2), pl.ds(6, 2)
    z_copy, to_right, to_left = [], [], []
    for h in halves:
        for d in range(3):
            rs_copy(h, d).wait()
        for lt in range(LT):
            text[h, 2 + lt] = (t_ref[lt, rows_of(h, x), :] + rs[h, 0, lt]) + (
                rs[h, 1, lt] + rs[h, 2, lt]
            )
        z_copy.append(remote(text.at[h, whole], zin.at[h, whole], 15, 15, partner, h))
        to_right += [
            remote(text.at[h, high], zin.at[h, before], 48, 48, right_far, h),
            remote(text.at[h, high], text.at[h, before], 22, 22, right, h),
        ]
        to_left += [
            remote(text.at[h, low], zin.at[h, after], 49, 49, left_far, h),
            remote(text.at[h, low], text.at[h, after], 23, 23, left, h),
        ]
        z_copy[h].start()

        @pl.when(has_right)
        def _():
            for copy in to_right[-2:]:
                copy.start()

        @pl.when(has_left)
        def _():
            for copy in to_left[-2:]:
                copy.start()

    halo_start(4)
    spread_rows(cf, tile, PAD + 16 * r - 1, 18, spread)
    begin_out()

    a_copy, a_keep, p_copy = [], [], []
    for h in halves:
        z_copy[h].wait_recv()

        @pl.when(has_left)
        def _():
            for copy in to_right[2 * h : 2 * h + 2]:
                copy.wait_recv()

        @pl.when(has_right)
        def _():
            for copy in to_left[2 * h : 2 * h + 2]:
                copy.wait_recv()

        for i in range(2):
            at = pl.ds(16 * i, 16)
            total = {g - 2: text[h, g, at, :] + zin[h, g, at, :] for g in range(8)}
            res = col_two_steps(total, cf, first)
            my_obs = oc[pl.ds(pl.multiple_of(128 * h + 32 * x + 16 * i, 16), 16), :]
            for lt in range(LT):
                ids = c * COLS + lt * GY + lax.broadcasted_iota(jnp.int32, (16, GY), 1)
                noise = jnp.broadcast_to(cf[5, pl.ds(first + lt, 1), :], (16, GY))
                psum[h, lt, at, :] = res[lt] + jnp.where(my_obs == ids, noise, 0.0)
        a_copy.append(remote(psum.at[h], pr.at[k, s, :, rows_of(h, x)], 28, 28, give_to, h))
        a_keep.append(
            pltpu.make_async_copy(psum.at[h], pr.at[k, s, :, rows_of(h, x)], local.at[13 + h])
        )
        pl.when(gives)(lambda: a_copy[h].start())
        pl.when(keeps)(lambda: a_keep[h].start())
    for h in halves:
        for d in range(3):
            p_copy.append(
                remote(psum.at[h], pc.at[:, rows_of(h, x)], 25 + d, 25 + d, x_peers[d], h)
            )
            p_copy[-1].start()
        for lt in range(LT):
            pc[lt, rows_of(h, x), :] = psum[h, lt]
    halo_start(5)

    hop2 = remote(relay1, relay2, 24, 24, partner)
    pl.when(at_edge)(lambda: keep1.wait())
    pl.when(no(at_edge))(lambda: hop1[0].wait_recv())
    hop2.start()
    transport(2)
    halo_start(6)

    t0 = jnp.where(holder, s, 1 - pair)
    kinds = (t0, 1 - t0)

    def part(h, i, d, kk):
        return pr.at[kk, kinds[i], :, rows_of(h, (y + 4 - d) % 4)]

    piece = [pr.at[k, s, :, rows_of(h, y)] for h in halves]
    a_wait = [remote(psum.at[h], piece[h], 28, 28, give_to, h) for h in halves]
    b_twin = [remote(piece[h], piece[h], 29, 30, twin_z, h) for h in halves]
    second = jnp.where(s == 1 - pair, 0, 1)
    b_near = [remote(piece[h], piece[h], 30, 29 + second, near_z, h) for h in halves]
    arrive = [
        [remote(part(h, i, 0, k), part(h, i, 0, k), 31 + i, 29 + i, far_z, h) for i in range(2)]
        for h in halves
    ]

    def along_y(h, i, d):
        n = 33 + 2 * d + i
        return remote(part(h, i, 0, k), part(h, i, 0, k), n, n, y_peers[d], h)

    def y_in(h, i, d):
        n = 33 + 2 * d + i
        return remote(part(h, i, d + 1, k), part(h, i, d + 1, k), n, n, y_peers[d], h)

    def to_core(h, i, d):
        n = 40 + 2 * d + i
        return remote(part(h, i, d, k), part(h, i, d, k), n, n, core, h)

    def core_in(h, i, d):
        n = 40 + 2 * d + i
        return remote(part(h, i, d, 1 - k), part(h, i, d, 1 - k), n, n, core, h)

    def pass_on(h, i):
        pl.when(near)(lambda: arrive[h][i].start())
        for d in range(3):
            along_y(h, i, d).start()
        to_core(h, i, 0).start()

    for h in halves:

        @pl.when(holder)
        def _():
            pl.when(takes)(lambda: a_wait[h].wait_recv())
            pl.when(no(takes))(lambda: a_keep[h].wait())
            b_near[h].start()
            b_twin[h].start()

        @pl.when(no(holder))
        def _():
            arrive[h][0].wait_recv()

        pass_on(h, 0)
    halo_start(7)
    for h in halves:
        arrive[h][1].wait_recv()
        pass_on(h, 1)

    transport(3)
    along_rows((1, 5), (2, 4))
    hop2.wait_recv()
    last = pltpu.make_async_copy(relay2, v.at[x, into], local.at[6])
    pl.when(at_edge)(lambda: last.start())

    def forward(j):
        return remote(relay2, v.at[j, into], 39, 52 + j, edge)

    for j in range(4):
        pl.when(no(at_edge) & (x == j))(lambda j=j: forward(j).start())

    for i in range(2):
        for h in halves:
            for d in range(3):
                y_in(h, i, d).wait_recv()
                to_core(h, i, d + 1).start()
        transport(4 + i)
        along_rows((5 + 2 * i, 7 + 2 * i), (4 + 2 * i, 6 + 2 * i))
    for copy in p_copy:
        copy.wait_recv()
    f = f_ref[...]
    gain = dot3(f, f, ((0,), (0,)))
    weights = dot3(gain, jnp.concatenate([pc[lt] for lt in range(LT)], axis=1), ((1,), (0,)))
    for i in range(2):
        subtract(k, i, weights)
    transport(6)
    along_rows((9, 11), (8, 10))
    for h in halves:
        for i in range(2):
            for d in range(4):
                core_in(h, i, d).wait_recv()
    for i in range(2):
        subtract(1 - k, i, weights)

    def store(n):
        rows = pl.ds(*((256, 1024), (1280, 768), (0, 256))[n])
        return pltpu.make_async_copy(out.at[:, rows], p_ref.at[:, rows], local.at[7 + n])

    store(0).start()
    transport(7)
    along_rows((11, 15), (10, 14))
    pl.when(down_near)(lambda: up_copy.wait_recv())
    pl.when(up_near)(lambda: down_copy.wait_recv())

    @pl.when(at_edge)
    def _():
        last.wait()
        for j in range(4):
            pl.when(x != j)(lambda j=j: forward(j).wait_recv())

    for flag, rows in ((r == 0, above), (r == 7, below)):

        @pl.when(flag)
        def _():
            for lt in range(LT):
                v[lt, rows, :] = jnp.zeros((256, GY), F32)

    along_rows((15, 17), (14, 16))
    store(1).start()
    along_rows((-1, 1), (0, 2))
    store(2).start()

    for n in range(3):
        store(n).wait()
    pl.when(up_near)(lambda: up_copy.wait_send())
    pl.when(down_near)(lambda: down_copy.wait_send())

    @pl.when(at_edge)
    def _():
        for j, copy in enumerate(hop1):
            pl.when(x != j)(lambda copy=copy: copy.wait_send())

    hop2.wait_send()
    pl.when(no(at_edge))(lambda: forward(0).wait_send())
    for copy in z_copy:
        copy.wait_send()

    @pl.when(has_right)
    def _():
        for copy in to_right:
            copy.wait_send()

    @pl.when(has_left)
    def _():
        for copy in to_left:
            copy.wait_send()

    for copy in p_copy:
        copy.wait_send()
    for h in halves:
        pl.when(gives)(lambda: a_copy[h].wait_send())
        pl.when(keeps & no(holder))(lambda: a_keep[h].wait())

        @pl.when(holder)
        def _():
            b_near[h].wait_send()
            b_twin[h].wait_send()

        for i in range(2):
            pl.when(near)(lambda: arrive[h][i].wait_send())
            for d in range(3):
                along_y(h, i, d).wait_send()
            for d in range(4):
                to_core(h, i, d).wait_send()
    for side in (0, 1):

        @pl.when(flags[side][0])
        def _():
            for n in range(len(PIECES)):
                for t in (0, 1):
                    halo_out(side, n, t).wait_send()


def kd(p_in, o_ref, p, sem, osem):
    chunks = [(lt, pl.ds(1024 * n, 1024)) for n in range(2) for lt in range(LT)]
    loads = [
        pltpu.make_async_copy(p_in.at[lt, at], p.at[lt, at], sem.at[n])
        for n, (lt, at) in enumerate(chunks)
    ]
    stores = [
        pltpu.make_async_copy(p.at[lt, at], o_ref.at[at, pl.ds(GY * lt, GY)], osem.at[n])
        for n, (lt, at) in enumerate(chunks)
    ]
    for copy in loads:
        copy.start()
    for load, put in zip(loads, stores):
        load.wait()
        put.start()
    for copy in stores:
        copy.wait()


def on_device(prior_cov, diffusivity, velocity, variance, observed_index, innov_factor):
    shape = jax.ShapeDtypeStruct
    limit = 60 * 1024 * 1024
    k = diffusivity.reshape(GX, GY)
    q = variance.reshape(GX, GY)
    p = pl.pallas_call(
        ka,
        out_shape=shape((LT, ROWS, GY), F32),
        in_specs=[ANY] + [VM] * 5,
        out_specs=ANY,
        scratch_shapes=[
            pltpu.VMEM((8, ROWS, GY), F32),
            pltpu.VMEM((LT, 2560, GY), F32),
            pltpu.VMEM((LT, 2304, GY), F32),
            pltpu.VMEM((LT, ROWS, GY), F32),
            pltpu.VMEM((5, 2304, GY), F32),
            pltpu.VMEM((8, GX + 2 * PAD, GY), F32),
            pltpu.VMEM((2, GX, GY), F32),
            pltpu.VMEM((8, GY), F32),
            pltpu.VMEM((NOBS, GY), jnp.int32),
            pltpu.VMEM((NOBS, ROWS), F32),
            pltpu.VMEM((LT, NOBS, GY), F32),
            pltpu.VMEM((LT, NOBS, GY), F32),
            pltpu.VMEM((2, 2, LT, NOBS, GY), F32),
            pltpu.VMEM((2, 3, LT, 32, GY), F32),
            pltpu.VMEM((2, LT, 32, GY), F32),
            pltpu.VMEM((2, 8, 32, GY), F32),
            pltpu.VMEM((2, 8, 32, GY), F32),
            pltpu.VMEM((256, GY), F32),
            pltpu.VMEM((256, GY), F32),
            pltpu.SemaphoreType.DMA((32,)),
            pltpu.SemaphoreType.DMA((32,)),
            pltpu.SemaphoreType.DMA((2, 56)),
            pltpu.SemaphoreType.DMA((2, 56)),
            pltpu.SemaphoreType.DMA((15,)),
        ],
        compiler_params=pltpu.CompilerParams(
            collective_id=0, has_side_effects=True, vmem_limit_bytes=limit
        ),
        name="exchange",
    )(prior_cov, observed_index.reshape(1, NOBS), k, velocity, q, innov_factor)
    return pl.pallas_call(
        kd,
        out_shape=shape((ROWS, COLS), F32),
        in_specs=[ANY],
        out_specs=ANY,
        scratch_shapes=[
            pltpu.VMEM((LT, ROWS, GY), F32),
            pltpu.SemaphoreType.DMA((8,)),
            pltpu.SemaphoreType.DMA((8,)),
        ],
        compiler_params=pltpu.CompilerParams(vmem_limit_bytes=limit),
        name="place",
    )(p)


def solution(mesh):
    return jax.shard_map(
        on_device,
        mesh=mesh,
        in_specs=(P("row", "col"), P(), P(), P(), P(), P()),
        out_specs=P("row", "col"),
        check_vma=False,
    )
```

time: 117 us -> 107 us (0.915)
  the two profiles are of different devices: /device:TPU:97 before, /device:TPU:2 now
where the time goes in v3:
time: 107 us
  Pallas kernels  107 us (100%)
    pallas_call x1, Pallas kernels, on_device(): pl.pallas_call(ka, out_shape=shape((LT, ROWS, GY), F32), in_specs=[ANY] +...  103 us
    pallas_call x1, Pallas kernels, on_device(): pl.pallas_call(kd, out_shape=shape((ROWS, COLS), F32), in_specs=[ANY], ou...  3.58 us

profile of v3, /device:TPU:2, one launch (start us, length us, event | category | flops | bytes accessed | tf_op | source)
XLA Modules:
  0.0 107.0 jit_solution(11204170619715239762)
XLA Ops:
  0.0 103.4 %exchange.1.p_in = f32[4,2048,128]{2,1,0:T(8,128)} custom-call(f32[2048,512]{1,0:T(8,128)} %c_ref.1, s32[1,256]{1,0:T(1,128)} %bitcast.5, f32[128,128]{1,0:T(8,128)} %bitcast.3, f32[2,16384]{1,0:T(2,128)} %vel_ref.1, f32[128,128]{1,0:T(8,128)} %bitcast.4, f32[256,256]{1,0:T(8,128)} %f_ref.1), custom_call_target="tpu_custom_call" | custom-call | tf_op jit(solution)/shard_map/exchange/pallas_call | solution.py:650
  103.5 3.6 %place.1 = f32[2048,512]{1,0:T(8,128)} custom-call(f32[4,2048,128]{2,1,0:T(8,128)} %exchange.1.p_in), custom_call_target="tpu_custom_call" | custom-call | tf_op jit(solution)/shard_map/place/pallas_call | solution.py:686

commit v4 on v3

--- a/solution.py
+++ b/solution.py
@@ -18,6 +18,7 @@
 MESH = pl.DeviceIdType.MESH
 PAD = 8
 VM = pl.BlockSpec(memory_space=pltpu.VMEM)
+HBM = pl.BlockSpec(memory_space=pltpu.HBM)
 ANY = pl.BlockSpec(memory_space=pl.ANY)
 
 
@@ -139,11 +140,10 @@
     vel_ref,
     q_ref,
     f_ref,
-    p_ref,
+    out,
     ext,
     v,
     v1,
-    out,
     spread,
     cf,
     speed,
@@ -173,9 +173,7 @@
     x_edge = jnp.where(zh == 0, 3, 0)
     has_left, has_right = c > 0, c < 31
     c_left, c_right = jnp.maximum(c - 1, 0), jnp.minimum(c + 1, 31)
-    r_far = 4 * (1 - zh) + x
-    left, right, partner = (r, c_left), (r, c_right), (r_far, c)
-    left_far, right_far = (r_far, c_left), (r_far, c_right)
+    left, right, partner = (r, c_left), (r, c_right), (4 * (1 - zh) + x, c)
     x_peers = [(4 * zh + (x + d) % 4, c) for d in (1, 2, 3)]
     y_peers = [(r, 8 * ((y + d) % 4) + 2 * zl + k) for d in (1, 2, 3)]
     z_peers = [(r, 8 * y + 2 * ((zl + d) % 4) + k) for d in (1, 2, 3)]
@@ -218,13 +216,13 @@
             pl.semaphore_signal(barrier, inc=1, device_id=device, device_id_type=MESH)
 
     greet(*x_peers, *y_peers, *z_peers, partner, core)
-    pl.when(has_left)(lambda: greet(left, left_far))
-    pl.when(has_right)(lambda: greet(right, right_far))
+    pl.when(has_left)(lambda: greet(left))
+    pl.when(has_right)(lambda: greet(right))
     pl.when(gives)(lambda: greet(give_to))
     pl.when(takes)(lambda: greet(take_from))
     one = lambda flag: jnp.where(flag, 1, 0)
     pl.semaphore_wait(
-        barrier, 11 + 2 * one(has_left) + 2 * one(has_right) + one(gives) + one(takes)
+        barrier, 11 + one(has_left) + one(has_right) + one(gives) + one(takes)
     )
 
     def halo_out(side, piece, t):
@@ -345,7 +343,6 @@
                 ext[t] = jnp.zeros((ROWS, GY), F32)
                 for h in halves:
                     text[h, t] = jnp.zeros((32, GY), F32)
-                    zin[h, t] = jnp.zeros((32, GY), F32)
 
     transport(0)
     transport(1)
@@ -381,48 +378,28 @@
             text[h, 2 + lt] = (t_ref[lt, rows_of(h, x), :] + rs[h, 0, lt]) + (
                 rs[h, 1, lt] + rs[h, 2, lt]
             )
-        z_copy.append(remote(text.at[h, whole], zin.at[h, whole], 15, 15, partner, h))
-        to_right += [
-            remote(text.at[h, high], zin.at[h, before], 48, 48, right_far, h),
-            remote(text.at[h, high], text.at[h, before], 22, 22, right, h),
-        ]
-        to_left += [
-            remote(text.at[h, low], zin.at[h, after], 49, 49, left_far, h),
-            remote(text.at[h, low], text.at[h, after], 23, 23, left, h),
-        ]
+        z_copy.append(remote(text.at[h, whole], zin.at[h], 15, 15, partner, h))
+        to_right.append(remote(text.at[h, high], text.at[h, before], 22, 22, right, h))
+        to_left.append(remote(text.at[h, low], text.at[h, after], 23, 23, left, h))
         z_copy[h].start()
-
-        @pl.when(has_right)
-        def _():
-            for copy in to_right[-2:]:
-                copy.start()
-
-        @pl.when(has_left)
-        def _():
-            for copy in to_left[-2:]:
-                copy.start()
 
     halo_start(4)
     spread_rows(cf, tile, PAD + 16 * r - 1, 18, spread)
+    for h in halves:
+        z_copy[h].wait()
+        for lt in range(LT):
+            text[h, 2 + lt] = text[h, 2 + lt] + zin[h, lt]
+        pl.when(has_right)(lambda: to_right[h].start())
+        pl.when(has_left)(lambda: to_left[h].start())
     begin_out()
 
     a_copy, a_keep, p_copy = [], [], []
     for h in halves:
-        z_copy[h].wait_recv()
-
-        @pl.when(has_left)
-        def _():
-            for copy in to_right[2 * h : 2 * h + 2]:
-                copy.wait_recv()
-
-        @pl.when(has_right)
-        def _():
-            for copy in to_left[2 * h : 2 * h + 2]:
-                copy.wait_recv()
-
+        pl.when(has_left)(lambda: to_right[h].wait_recv())
+        pl.when(has_right)(lambda: to_left[h].wait_recv())
         for i in range(2):
             at = pl.ds(16 * i, 16)
-            total = {g - 2: text[h, g, at, :] + zin[h, g, at, :] for g in range(8)}
+            total = {g - 2: text[h, g, at, :] for g in range(8)}
             res = col_two_steps(total, cf, first)
             my_obs = oc[pl.ds(pl.multiple_of(128 * h + 32 * x + 16 * i, 16), 16), :]
             for lt in range(LT):
@@ -443,14 +420,12 @@
             p_copy[-1].start()
         for lt in range(LT):
             pc[lt, rows_of(h, x), :] = psum[h, lt]
-    halo_start(5)
 
     hop2 = remote(relay1, relay2, 24, 24, partner)
     pl.when(at_edge)(lambda: keep1.wait())
     pl.when(no(at_edge))(lambda: hop1[0].wait_recv())
     hop2.start()
     transport(2)
-    halo_start(6)
 
     t0 = jnp.where(holder, s, 1 - pair)
     kinds = (t0, 1 - t0)
@@ -504,10 +479,13 @@
             arrive[h][0].wait_recv()
 
         pass_on(h, 0)
-    halo_start(7)
+    halo_start(5)
     for h in halves:
         arrive[h][1].wait_recv()
         pass_on(h, 1)
+
+    halo_start(6)
+    halo_start(7)
 
     transport(3)
     along_rows((1, 5), (2, 4))
@@ -544,13 +522,6 @@
     for i in range(2):
         subtract(1 - k, i, weights)
 
-    def store(n):
-        rows = pl.ds(*((256, 1024), (1280, 768), (0, 256))[n])
-        return pltpu.make_async_copy(out.at[:, rows], p_ref.at[:, rows], local.at[7 + n])
-
-    store(0).start()
-    transport(7)
-    along_rows((11, 15), (10, 14))
     pl.when(down_near)(lambda: up_copy.wait_recv())
     pl.when(up_near)(lambda: down_copy.wait_recv())
 
@@ -567,13 +538,11 @@
             for lt in range(LT):
                 v[lt, rows, :] = jnp.zeros((256, GY), F32)
 
+    along_rows((-1, 1), (0, 2))
+    transport(7)
+    along_rows((11, 15), (10, 14))
     along_rows((15, 17), (14, 16))
-    store(1).start()
-    along_rows((-1, 1), (0, 2))
-    store(2).start()
-
-    for n in range(3):
-        store(n).wait()
+
     pl.when(up_near)(lambda: up_copy.wait_send())
     pl.when(down_near)(lambda: down_copy.wait_send())
 
@@ -584,8 +553,6 @@
 
     hop2.wait_send()
     pl.when(no(at_edge))(lambda: forward(0).wait_send())
-    for copy in z_copy:
-        copy.wait_send()
 
     @pl.when(has_right)
     def _():
@@ -623,40 +590,31 @@
                     halo_out(side, n, t).wait_send()
 
 
-def kd(p_in, o_ref, p, sem, osem):
-    chunks = [(lt, pl.ds(1024 * n, 1024)) for n in range(2) for lt in range(LT)]
-    loads = [
-        pltpu.make_async_copy(p_in.at[lt, at], p.at[lt, at], sem.at[n])
-        for n, (lt, at) in enumerate(chunks)
+def kd(p_ref, o_ref, sem):
+    stores = [
+        pltpu.make_async_copy(p_ref.at[lt], o_ref.at[:, pl.ds(GY * lt, GY)], sem.at[lt])
+        for lt in range(LT)
     ]
-    stores = [
-        pltpu.make_async_copy(p.at[lt, at], o_ref.at[at, pl.ds(GY * lt, GY)], osem.at[n])
-        for n, (lt, at) in enumerate(chunks)
-    ]
-    for copy in loads:
+    for copy in stores:
         copy.start()
-    for load, put in zip(loads, stores):
-        load.wait()
-        put.start()
     for copy in stores:
         copy.wait()
 
 
 def on_device(prior_cov, diffusivity, velocity, variance, observed_index, innov_factor):
     shape = jax.ShapeDtypeStruct
-    limit = 60 * 1024 * 1024
+    limit = 48 * 1024 * 1024
     k = diffusivity.reshape(GX, GY)
     q = variance.reshape(GX, GY)
     p = pl.pallas_call(
         ka,
         out_shape=shape((LT, ROWS, GY), F32),
-        in_specs=[ANY] + [VM] * 5,
-        out_specs=ANY,
+        in_specs=[HBM] + [VM] * 5,
+        out_specs=VM,
         scratch_shapes=[
             pltpu.VMEM((8, ROWS, GY), F32),
             pltpu.VMEM((LT, 2560, GY), F32),
             pltpu.VMEM((LT, 2304, GY), F32),
-            pltpu.VMEM((LT, ROWS, GY), F32),
             pltpu.VMEM((5, 2304, GY), F32),
             pltpu.VMEM((8, GX + 2 * PAD, GY), F32),
             pltpu.VMEM((2, GX, GY), F32),
@@ -668,7 +626,7 @@
             pltpu.VMEM((2, 2, LT, NOBS, GY), F32),
             pltpu.VMEM((2, 3, LT, 32, GY), F32),
             pltpu.VMEM((2, LT, 32, GY), F32),
-            pltpu.VMEM((2, 8, 32, GY), F32),
+            pltpu.VMEM((2, LT, 32, GY), F32),
             pltpu.VMEM((2, 8, 32, GY), F32),
             pltpu.VMEM((256, GY), F32),
             pltpu.VMEM((256, GY), F32),
@@ -686,14 +644,10 @@
     return pl.pallas_call(
         kd,
         out_shape=shape((ROWS, COLS), F32),
-        in_specs=[ANY],
+        in_specs=[VM],
         out_specs=ANY,
-        scratch_shapes=[
-            pltpu.VMEM((LT, ROWS, GY), F32),
-            pltpu.SemaphoreType.DMA((8,)),
-            pltpu.SemaphoreType.DMA((8,)),
-        ],
-        compiler_params=pltpu.CompilerParams(vmem_limit_bytes=limit),
+        scratch_shapes=[pltpu.SemaphoreType.DMA((LT,))],
+        compiler_params=pltpu.CompilerParams(vmem_limit_bytes=8 * 1024 * 1024),
         name="place",
     )(p)
 

time: 107 us -> 101 us (0.944)
  Pallas kernels: 107 us -> 96.9 us
  local copies, waits for them, and re-layouts: 0 us -> 4.21 us
    pallas_call x2, Pallas kernels: 107 us -> 96.9 us  [the longest x1 94.8 us: on_device(): pl.pallas_call(ka, out_shape=shape((LT, ROWS, GY), F32), in_specs=[HBM] +...]
    unnamed x0 -> x10, local copies, waits for them, and re-layouts: none -> 4.21 us
where the time goes in v4:
time: 101 us
  Pallas kernels  96.9 us (96%)
  local copies, waits for them, and re-layouts  4.21 us (4%)
    pallas_call x1, Pallas kernels, on_device(): pl.pallas_call(ka, out_shape=shape((LT, ROWS, GY), F32), in_specs=[HBM] +...  94.8 us
    unnamed x10, local copies, waits for them, and re-layouts  4.21 us
    pallas_call x1, Pallas kernels, on_device(): pl.pallas_call(kd, out_shape=shape((ROWS, COLS), F32), in_specs=[VM], out...  2.04 us

profile of v4, /device:TPU:2, one launch (start us, length us, event | category | flops | bytes accessed | tf_op | source)
XLA Modules:
  0.0 101.1 jit_solution(10369453724451886210)
XLA Ops:
  0.0 0.0 copy-start
  0.0 0.9 copy-done
  1.0 0.0 copy-start.1
  1.0 0.9 copy-done.1
  1.9 0.0 copy-start.2
  1.9 0.8 copy-done.2
  2.7 0.0 copy-start.3
  2.7 0.8 copy-done.3
  3.5 0.0 copy-start.4
  3.5 0.7 copy-done.4
  4.2 94.8 %exchange.1.p_ref = f32[4,2048,128]{2,1,0:T(8,128)S(1)} custom-call(f32[2048,512]{1,0:T(8,128)} %c_ref.1, s32[1,256]{1,0:T(1,128)S(1)} %bitcast.5, f32[128,128]{1,0:T(8,128)S(1)} %bitcast.3, f32[2,16384]{1,0:T(2,128)S(1)} %copy-done.1, f32[128,128]{1,0:T(8,128)S(1)} %bitcast.4, f32[256,256]{1,0:T(8,128)S(1)} %copy-done), custom_call_target="tpu_custom_call" | custom-call | tf_op jit(solution)/shard_map/exchange/pallas_call | solution.py:609
  99.0 2.0 %place.1 = f32[2048,512]{1,0:T(8,128)} custom-call(f32[4,2048,128]{2,1,0:T(8,128)S(1)} %exchange.1.p_ref), custom_call_target="tpu_custom_call" | custom-call | tf_op jit(solution)/shard_map/place/pallas_call | solution.py:644
Async XLA Ops:
  0.0 0.9 copy-start
  1.0 0.9 copy-start.1
  1.9 0.8 copy-start.2
  2.7 0.8 copy-start.3
  3.5 0.7 copy-start.4

commit v5 on v4

--- a/solution.py
+++ b/solution.py
@@ -18,7 +18,6 @@
 MESH = pl.DeviceIdType.MESH
 PAD = 8
 VM = pl.BlockSpec(memory_space=pltpu.VMEM)
-HBM = pl.BlockSpec(memory_space=pltpu.HBM)
 ANY = pl.BlockSpec(memory_space=pl.ANY)
 
 
@@ -140,10 +139,11 @@
     vel_ref,
     q_ref,
     f_ref,
-    out,
+    p_ref,
     ext,
     v,
     v1,
+    out,
     spread,
     cf,
     speed,
@@ -522,6 +522,13 @@
     for i in range(2):
         subtract(1 - k, i, weights)
 
+    def store(n):
+        rows = pl.ds(*((256, 1024), (1280, 768), (0, 256))[n])
+        return pltpu.make_async_copy(out.at[:, rows], p_ref.at[:, rows], local.at[7 + n])
+
+    store(0).start()
+    transport(7)
+    along_rows((11, 15), (10, 14))
     pl.when(down_near)(lambda: up_copy.wait_recv())
     pl.when(up_near)(lambda: down_copy.wait_recv())
 
@@ -538,11 +545,13 @@
             for lt in range(LT):
                 v[lt, rows, :] = jnp.zeros((256, GY), F32)
 
+    along_rows((15, 17), (14, 16))
+    store(1).start()
     along_rows((-1, 1), (0, 2))
-    transport(7)
-    along_rows((11, 15), (10, 14))
-    along_rows((15, 17), (14, 16))
-
+    store(2).start()
+
+    for n in range(3):
+        store(n).wait()
     pl.when(up_near)(lambda: up_copy.wait_send())
     pl.when(down_near)(lambda: down_copy.wait_send())
 
@@ -590,31 +599,40 @@
                     halo_out(side, n, t).wait_send()
 
 
-def kd(p_ref, o_ref, sem):
+def kd(p_in, o_ref, p, sem, osem):
+    chunks = [(lt, pl.ds(1024 * n, 1024)) for n in range(2) for lt in range(LT)]
+    loads = [
+        pltpu.make_async_copy(p_in.at[lt, at], p.at[lt, at], sem.at[n])
+        for n, (lt, at) in enumerate(chunks)
+    ]
     stores = [
-        pltpu.make_async_copy(p_ref.at[lt], o_ref.at[:, pl.ds(GY * lt, GY)], sem.at[lt])
-        for lt in range(LT)
+        pltpu.make_async_copy(p.at[lt, at], o_ref.at[at, pl.ds(GY * lt, GY)], osem.at[n])
+        for n, (lt, at) in enumerate(chunks)
     ]
-    for copy in stores:
+    for copy in loads:
         copy.start()
+    for load, put in zip(loads, stores):
+        load.wait()
+        put.start()
     for copy in stores:
         copy.wait()
 
 
 def on_device(prior_cov, diffusivity, velocity, variance, observed_index, innov_factor):
     shape = jax.ShapeDtypeStruct
-    limit = 48 * 1024 * 1024
+    limit = 60 * 1024 * 1024
     k = diffusivity.reshape(GX, GY)
     q = variance.reshape(GX, GY)
     p = pl.pallas_call(
         ka,
         out_shape=shape((LT, ROWS, GY), F32),
-        in_specs=[HBM] + [VM] * 5,
-        out_specs=VM,
+        in_specs=[ANY] + [VM] * 5,
+        out_specs=ANY,
         scratch_shapes=[
             pltpu.VMEM((8, ROWS, GY), F32),
             pltpu.VMEM((LT, 2560, GY), F32),
             pltpu.VMEM((LT, 2304, GY), F32),
+            pltpu.VMEM((LT, ROWS, GY), F32),
             pltpu.VMEM((5, 2304, GY), F32),
             pltpu.VMEM((8, GX + 2 * PAD, GY), F32),
             pltpu.VMEM((2, GX, GY), F32),
@@ -644,10 +662,14 @@
     return pl.pallas_call(
         kd,
         out_shape=shape((ROWS, COLS), F32),
-        in_specs=[VM],
+        in_specs=[ANY],
         out_specs=ANY,
-        scratch_shapes=[pltpu.SemaphoreType.DMA((LT,))],
-        compiler_params=pltpu.CompilerParams(vmem_limit_bytes=8 * 1024 * 1024),
+        scratch_shapes=[
+            pltpu.VMEM((LT, ROWS, GY), F32),
+            pltpu.SemaphoreType.DMA((8,)),
+            pltpu.SemaphoreType.DMA((8,)),
+        ],
+        compiler_params=pltpu.CompilerParams(vmem_limit_bytes=limit),
         name="place",
     )(p)
 

time: 101 us -> 100 us (0.990)
  local copies, waits for them, and re-layouts: 4.21 us -> 0 us
  Pallas kernels: 96.9 us -> 100 us
    unnamed x10 -> x0, local copies, waits for them, and re-layouts: 4.21 us -> none
    pallas_call x2, Pallas kernels: 96.9 us -> 100 us  [the longest x1 96.6 us: on_device(): pl.pallas_call(ka, out_shape=shape((LT, ROWS, GY), F32), in_specs=[ANY] +...]
where the time goes in v5:
time: 100 us
  Pallas kernels  100 us (100%)
    pallas_call x1, Pallas kernels, on_device(): pl.pallas_call(ka, out_shape=shape((LT, ROWS, GY), F32), in_specs=[ANY] +...  96.6 us
    pallas_call x1, Pallas kernels, on_device(): pl.pallas_call(kd, out_shape=shape((ROWS, COLS), F32), in_specs=[ANY], ou...  3.58 us

profile of v5, /device:TPU:2, one launch (start us, length us, event | category | flops | bytes accessed | tf_op | source)
XLA Modules:
  0.0 100.2 jit_solution(14298904318864519222)
XLA Ops:
  0.0 96.6 %exchange.1.p_in = f32[4,2048,128]{2,1,0:T(8,128)} custom-call(f32[2048,512]{1,0:T(8,128)} %c_ref.1, s32[1,256]{1,0:T(1,128)} %bitcast.5, f32[128,128]{1,0:T(8,128)} %bitcast.3, f32[2,16384]{1,0:T(2,128)} %vel_ref.1, f32[128,128]{1,0:T(8,128)} %bitcast.4, f32[256,256]{1,0:T(8,128)} %f_ref.1), custom_call_target="tpu_custom_call" | custom-call | tf_op jit(solution)/shard_map/exchange/pallas_call | solution.py:626
  96.6 3.6 %place.1 = f32[2048,512]{1,0:T(8,128)} custom-call(f32[4,2048,128]{2,1,0:T(8,128)} %exchange.1.p_in), custom_call_target="tpu_custom_call" | custom-call | tf_op jit(solution)/shard_map/place/pallas_call | solution.py:662
